TPU v7x, 128 devices: a whole 4x4x4 slice. The times are simulated.
128 devices in a mesh: pipe: 8 (over x, y_lo), dp: 16 (over y_hi, z, core).
Axes of the slice: x: 4, y: 4 (y_hi: 2, y_lo: 2; y = y_hi * 2 + y_lo), z: 4, core: 2. Of those that a mesh axis runs over, the one named last changes fastest.
Arguments:
- inputs: bfloat16 [6, 512, 8192], P(None, 'dp'), may hold values from -6 to 6
- cotangent: bfloat16 [6, 512, 8192], P(None, 'dp'), may hold values from -0.19921875 to 0.19921875
- plan_order: int32 [6], replicated, may hold values from 0 to 5, each once
- norm_gain: float32 [8, 8192], P('pipe'), may hold values from 0.5 to 1.5
- weight_in: bfloat16 [8, 8192, 512], P('pipe'), may hold values from -0.0625 to 0.0625
- weight_out: bfloat16 [8, 512, 8192], P('pipe'), may hold values from -0.25 to 0.25
Outputs:
- grad_in: bfloat16 [8, 8192, 512], P('pipe', 'dp')
- grad_out: bfloat16 [8, 512, 8192], P('pipe', None, 'dp')
Inputs may be any that keep to these rules, and one draw needn't show every extreme that they name: plan_order names each slot's sample once: a permutation.
All inputs are finite; a program needn't handle non-finite values.
Results may differ from a plain program's by a relative error of at most 0.024.
Values may be sent and summed in bfloat16 or wider, within the bound.
No kernel may reach another device: no remote copies, remote signals or barrier semaphores. Data moves between devices by JAX's collectives and lax.ppermute only.
A program may use at most 128 MiB of HBM per device.

v0:
```python
import jax
import jax.numpy as jnp
from jax import lax
from jax.sharding import PartitionSpec as P

EPSILON = 1e-05


def passed_along(value, axis, by):
    length = lax.axis_size(axis)
    pairs = [(i, i + by) for i in range(length) if 0 <= i + by < length]
    return lax.ppermute(value, axis, pairs)


def sent_together(arrays, axis, dim, along):
    widths = [a.shape[along] for a in arrays]
    both = jnp.concatenate(arrays, axis=along)
    result = lax.all_gather(both, axis, axis=dim, tiled=True)
    return tuple(jnp.split(result, [sum(widths[:k]) for k in range(1, len(widths))], axis=along))


def inner_section(rows_in, gain_row, weight_first):
    float_cast = rows_in.astype(jnp.float32)
    inverse_root_mean = lax.rsqrt(
        jnp.mean(float_cast * float_cast, axis=-1, keepdims=True) + EPSILON
    )
    normed = (float_cast * inverse_root_mean * gain_row).astype(jnp.bfloat16)
    pre_act = jnp.dot(normed, weight_first, preferred_element_type=jnp.float32)
    hidden = jax.nn.silu(pre_act).astype(jnp.bfloat16)
    return (float_cast, inverse_root_mean, normed, pre_act, hidden)


def backward_section(
    float_cast, inverse_root_mean, pre_act, incoming_gradient, gain_row, weight_first, weight_second
):
    grad_hidden = jnp.einsum(
        "td,rd->tr", incoming_gradient, weight_second, preferred_element_type=jnp.float32
    )
    sigmoid_pre = jax.nn.sigmoid(pre_act)
    grad_pre = (grad_hidden * sigmoid_pre * (1.0 + pre_act * (1.0 - sigmoid_pre))).astype(
        jnp.bfloat16
    )
    back_rows = jnp.einsum("tr,dr->td", grad_pre, weight_first, preferred_element_type=jnp.float32)
    normalized_input = float_cast * inverse_root_mean
    rescaled_rows = back_rows * gain_row
    grad_rows = incoming_gradient.astype(jnp.float32) + inverse_root_mean * (
        rescaled_rows
        - normalized_input * jnp.mean(rescaled_rows * normalized_input, axis=-1, keepdims=True)
    )
    return (grad_rows.astype(jnp.bfloat16), grad_pre)


def pick_slot(buffer, slot_index):
    return lax.dynamic_index_in_dim(buffer, slot_index, 0, keepdims=False)


def put_slot(buffer, new_value, slot_index, active_flag):
    previous = pick_slot(buffer, slot_index)
    return lax.dynamic_update_index_in_dim(
        buffer, jnp.where(active_flag, new_value, previous), slot_index, 0
    )


def per_device(inputs, cotangent, plan_order, norm_gain, weight_in, weight_out):
    gain_row = norm_gain[0]
    weight_first = weight_in[0]
    weight_second = weight_out[0]
    sections = lax.axis_size("pipe")
    section_index = lax.axis_index("pipe")
    micro_count, row_count, model_width = inputs.shape
    inner_width = weight_first.shape[1]
    tick_count = micro_count + sections - 1

    def buffer(columns, dtype):
        return jnp.zeros((micro_count, row_count, columns), dtype)

    extras = ()

    def forward_tick(moment, state_tuple):
        outgoing, kept_rows, kept_extra = state_tuple
        arrived = passed_along(outgoing, "pipe", 1)
        position = moment - section_index
        active_flag = (position >= 0) & (position < micro_count)
        slot_index = jnp.clip(position, 0, micro_count - 1)
        fresh_rows = pick_slot(inputs, plan_order[slot_index])
        rows_in = jnp.where(section_index == 0, fresh_rows, arrived)
        float_cast, inverse_root_mean, normed, pre_act, hidden = inner_section(
            rows_in, gain_row, weight_first
        )
        result = (
            float_cast + jnp.dot(hidden, weight_second, preferred_element_type=jnp.float32)
        ).astype(jnp.bfloat16)
        kept_rows = put_slot(kept_rows, rows_in, slot_index, active_flag)
        return (result, kept_rows, kept_extra)

    empty_rows = jnp.zeros((row_count, model_width), jnp.bfloat16)
    unused, kept_rows, extras = lax.fori_loop(
        0, tick_count, forward_tick, (empty_rows, buffer(model_width, jnp.bfloat16), extras)
    )
    normed_start = buffer(model_width, jnp.bfloat16)
    hidden_start = buffer(inner_width, jnp.bfloat16)

    def backward_tick(moment, state_tuple):
        outgoing, normed_all, hidden_gathered, grad_all, upstream_all = state_tuple
        arrived = passed_along(outgoing, "pipe", -1)
        position = moment - (sections - 1 - section_index)
        active_flag = (position >= 0) & (position < micro_count)
        slot_index = jnp.clip(position, 0, micro_count - 1)
        incoming_gradient = jnp.where(
            section_index == sections - 1, pick_slot(cotangent, slot_index), arrived
        )
        rows_in = pick_slot(kept_rows, slot_index)
        float_cast, inverse_root_mean, normed, pre_act, hidden = inner_section(
            rows_in, gain_row, weight_first
        )
        normed_all = put_slot(normed_all, normed, slot_index, active_flag)
        hidden_gathered = put_slot(hidden_gathered, hidden, slot_index, active_flag)
        grad_rows, grad_pre = backward_section(
            float_cast,
            inverse_root_mean,
            pre_act,
            incoming_gradient,
            gain_row,
            weight_first,
            weight_second,
        )
        grad_all = put_slot(grad_all, grad_pre, slot_index, active_flag)
        upstream_all = put_slot(upstream_all, incoming_gradient, slot_index, active_flag)
        return (grad_rows, normed_all, hidden_gathered, grad_all, upstream_all)

    start_state = (
        empty_rows,
        normed_start,
        hidden_start,
        buffer(inner_width, jnp.bfloat16),
        buffer(model_width, jnp.bfloat16),
    )
    unused, normed_all, hidden_gathered, grad_all, upstream_all = lax.fori_loop(
        0, tick_count, backward_tick, start_state
    )
    tokens = micro_count * row_count
    normed_flat = normed_all.reshape(tokens, model_width)
    hidden_flat = hidden_gathered.reshape(tokens, inner_width)
    grad_flat = grad_all.reshape(tokens, inner_width)
    upstream_flat = upstream_all.reshape(tokens, model_width)
    sources = lax.axis_size("dp")
    normed_cols, upstream_cols = (
        lax.all_to_all(normed_flat, "dp", split_axis=1, concat_axis=0, tiled=True),
        lax.all_to_all(upstream_flat, "dp", split_axis=1, concat_axis=0, tiled=True),
    )
    gradient_rows_gathered, hidden_rows_all = sent_together((grad_flat, hidden_flat), "dp", 0, 1)

    def grouped(array):
        return array.reshape(sources, tokens, array.shape[-1])

    partial_input = jnp.einsum(
        "qtd,qtr->qdr",
        grouped(normed_cols),
        grouped(gradient_rows_gathered),
        preferred_element_type=jnp.float32,
    )
    part_out = jnp.einsum(
        "qtr,qtd->qrd",
        grouped(hidden_rows_all),
        grouped(upstream_cols),
        preferred_element_type=jnp.float32,
    )
    total_in = jnp.sum(
        lax.optimization_barrier(partial_input.astype(jnp.bfloat16)).astype(jnp.float32), axis=0
    )
    total_out = jnp.sum(
        lax.optimization_barrier(part_out.astype(jnp.bfloat16)).astype(jnp.float32), axis=0
    )
    return (total_in.astype(jnp.bfloat16)[None], total_out.astype(jnp.bfloat16)[None])


def solution(mesh):
    in_specs = (
        P(None, "dp", None),
        P(None, "dp", None),
        P(),
        P("pipe", None),
        P("pipe", None, None),
        P("pipe", None, None),
    )
    out_specs = (P("pipe", "dp", None), P("pipe", None, "dp"))
    return jax.shard_map(
        per_device, mesh=mesh, in_specs=in_specs, out_specs=out_specs, check_vma=False
    )
```

profile of v0, /device:TPU:1, one launch (start us, length us, event | category | flops | bytes accessed | tf_op | source)
XLA Modules:
  0.0 831.1 jit_solution(2650859283386387271)
XLA Ops:
  9.2 299.6 %while.41 = (s32[]{:T(128)}, bf16[32,8192]{1,0:T(8,128)(2,1)S(1)}, bf16[6,32,8192]{2,1,0:T(8,128)(2,1)}, pred[]{:T(512)}, s32[]{:T(128)}, /*index=5*/s32[6]{0:T(...) while((s32[]{:T(128)}, bf16[32,8192]{1,0:T(8,128)(2,1)S(1)}, ...), condition=%wide.region_2.3_spmd.clone, body=%wide.region_0.2_spmd.clone.sunk | while | flops 540360768 | bytes 25199916 | solution.py:97
  16.9 7.0 collective-permute-done
  26.2 8.9 %fusion.69 = bf16[32,8192]{1,0:T(8,128)(2,1)S(1)} fusion(bf16[512,8192]{1,0:T(8,128)(2,1)} %get-tuple-element.827, bf16[32,8192]{1,0:T(8,128)(2,1)S(1)} %get-tuple-element.763, bf16[8192,512]{1,0:T(8,128)(2,1)} %get-tuple-element.826, f32[8192]{0:T(1024)S(1)} %bitcast.141, f32[32]{0:T(128)S(1)} %add_rsqrt_fusion.4), kind=kOutput, calls=%fused_computation.1.clone.1 | convolution fusion | flops 538787840 | bytes 17858688 | tf_op jit(solution)/shard_map/while/body/eval_jaxpr/dot_general | solution.py:91
  42.9 6.0 collective-permute-done
  51.2 8.9 %fusion.69 = bf16[32,8192]{1,0:T(8,128)(2,1)S(1)} fusion(bf16[512,8192]{1,0:T(8,128)(2,1)} %get-tuple-element.827, bf16[32,8192]{1,0:T(8,128)(2,1)S(1)} %get-tuple-element.763, bf16[8192,512]{1,0:T(8,128)(2,1)} %get-tuple-element.826, f32[8192]{0:T(1024)S(1)} %bitcast.141, f32[32]{0:T(128)S(1)} %add_rsqrt_fusion.4), kind=kOutput, calls=%fused_computation.1.clone.1 | convolution fusion | flops 538787840 | bytes 17858688 | tf_op jit(solution)/shard_map/while/body/eval_jaxpr/dot_general | solution.py:91
  75.4 8.9 %fusion.69 = bf16[32,8192]{1,0:T(8,128)(2,1)S(1)} fusion(bf16[512,8192]{1,0:T(8,128)(2,1)} %get-tuple-element.827, bf16[32,8192]{1,0:T(8,128)(2,1)S(1)} %get-tuple-element.763, bf16[8192,512]{1,0:T(8,128)(2,1)} %get-tuple-element.826, f32[8192]{0:T(1024)S(1)} %bitcast.141, f32[32]{0:T(128)S(1)} %add_rsqrt_fusion.4), kind=kOutput, calls=%fused_computation.1.clone.1 | convolution fusion | flops 538787840 | bytes 17858688 | tf_op jit(solution)/shard_map/while/body/eval_jaxpr/dot_general | solution.py:91
  99.2 8.9 %fusion.69 = bf16[32,8192]{1,0:T(8,128)(2,1)S(1)} fusion(bf16[512,8192]{1,0:T(8,128)(2,1)} %get-tuple-element.827, bf16[32,8192]{1,0:T(8,128)(2,1)S(1)} %get-tuple-element.763, bf16[8192,512]{1,0:T(8,128)(2,1)} %get-tuple-element.826, f32[8192]{0:T(1024)S(1)} %bitcast.141, f32[32]{0:T(128)S(1)} %add_rsqrt_fusion.4), kind=kOutput, calls=%fused_computation.1.clone.1 | convolution fusion | flops 538787840 | bytes 17858688 | tf_op jit(solution)/shard_map/while/body/eval_jaxpr/dot_general | solution.py:91
  122.4 8.9 %fusion.69 = bf16[32,8192]{1,0:T(8,128)(2,1)S(1)} fusion(bf16[512,8192]{1,0:T(8,128)(2,1)} %get-tuple-element.827, bf16[32,8192]{1,0:T(8,128)(2,1)S(1)} %get-tuple-element.763, bf16[8192,512]{1,0:T(8,128)(2,1)} %get-tuple-element.826, f32[8192]{0:T(1024)S(1)} %bitcast.141, f32[32]{0:T(128)S(1)} %add_rsqrt_fusion.4), kind=kOutput, calls=%fused_computation.1.clone.1 | convolution fusion | flops 538787840 | bytes 17858688 | tf_op jit(solution)/shard_map/while/body/eval_jaxpr/dot_general | solution.py:91
  144.8 8.9 %fusion.69 = bf16[32,8192]{1,0:T(8,128)(2,1)S(1)} fusion(bf16[512,8192]{1,0:T(8,128)(2,1)} %get-tuple-element.827, bf16[32,8192]{1,0:T(8,128)(2,1)S(1)} %get-tuple-element.763, bf16[8192,512]{1,0:T(8,128)(2,1)} %get-tuple-element.826, f32[8192]{0:T(1024)S(1)} %bitcast.141, f32[32]{0:T(128)S(1)} %add_rsqrt_fusion.4), kind=kOutput, calls=%fused_computation.1.clone.1 | convolution fusion | flops 538787840 | bytes 17858688 | tf_op jit(solution)/shard_map/while/body/eval_jaxpr/dot_general | solution.py:91
  167.2 8.9 %fusion.69 = bf16[32,8192]{1,0:T(8,128)(2,1)S(1)} fusion(bf16[512,8192]{1,0:T(8,128)(2,1)} %get-tuple-element.827, bf16[32,8192]{1,0:T(8,128)(2,1)S(1)} %get-tuple-element.763, bf16[8192,512]{1,0:T(8,128)(2,1)} %get-tuple-element.826, f32[8192]{0:T(1024)S(1)} %bitcast.141, f32[32]{0:T(128)S(1)} %add_rsqrt_fusion.4), kind=kOutput, calls=%fused_computation.1.clone.1 | convolution fusion | flops 538787840 | bytes 17858688 | tf_op jit(solution)/shard_map/while/body/eval_jaxpr/dot_general | solution.py:91
  189.3 8.9 %fusion.69 = bf16[32,8192]{1,0:T(8,128)(2,1)S(1)} fusion(bf16[512,8192]{1,0:T(8,128)(2,1)} %get-tuple-element.827, bf16[32,8192]{1,0:T(8,128)(2,1)S(1)} %get-tuple-element.763, bf16[8192,512]{1,0:T(8,128)(2,1)} %get-tuple-element.826, f32[8192]{0:T(1024)S(1)} %bitcast.141, f32[32]{0:T(128)S(1)} %add_rsqrt_fusion.4), kind=kOutput, calls=%fused_computation.1.clone.1 | convolution fusion | flops 538787840 | bytes 17858688 | tf_op jit(solution)/shard_map/while/body/eval_jaxpr/dot_general | solution.py:91
  211.4 8.9 %fusion.69 = bf16[32,8192]{1,0:T(8,128)(2,1)S(1)} fusion(bf16[512,8192]{1,0:T(8,128)(2,1)} %get-tuple-element.827, bf16[32,8192]{1,0:T(8,128)(2,1)S(1)} %get-tuple-element.763, bf16[8192,512]{1,0:T(8,128)(2,1)} %get-tuple-element.826, f32[8192]{0:T(1024)S(1)} %bitcast.141, f32[32]{0:T(128)S(1)} %add_rsqrt_fusion.4), kind=kOutput, calls=%fused_computation.1.clone.1 | convolution fusion | flops 538787840 | bytes 17858688 | tf_op jit(solution)/shard_map/while/body/eval_jaxpr/dot_general | solution.py:91
  233.5 8.9 %fusion.69 = bf16[32,8192]{1,0:T(8,128)(2,1)S(1)} fusion(bf16[512,8192]{1,0:T(8,128)(2,1)} %get-tuple-element.827, bf16[32,8192]{1,0:T(8,128)(2,1)S(1)} %get-tuple-element.763, bf16[8192,512]{1,0:T(8,128)(2,1)} %get-tuple-element.826, f32[8192]{0:T(1024)S(1)} %bitcast.141, f32[32]{0:T(128)S(1)} %add_rsqrt_fusion.4), kind=kOutput, calls=%fused_computation.1.clone.1 | convolution fusion | flops 538787840 | bytes 17858688 | tf_op jit(solution)/shard_map/while/body/eval_jaxpr/dot_general | solution.py:91
  255.6 8.9 %fusion.69 = bf16[32,8192]{1,0:T(8,128)(2,1)S(1)} fusion(bf16[512,8192]{1,0:T(8,128)(2,1)} %get-tuple-element.827, bf16[32,8192]{1,0:T(8,128)(2,1)S(1)} %get-tuple-element.763, bf16[8192,512]{1,0:T(8,128)(2,1)} %get-tuple-element.826, f32[8192]{0:T(1024)S(1)} %bitcast.141, f32[32]{0:T(128)S(1)} %add_rsqrt_fusion.4), kind=kOutput, calls=%fused_computation.1.clone.1 | convolution fusion | flops 538787840 | bytes 17858688 | tf_op jit(solution)/shard_map/while/body/eval_jaxpr/dot_general | solution.py:91
  277.8 8.9 %fusion.69 = bf16[32,8192]{1,0:T(8,128)(2,1)S(1)} fusion(bf16[512,8192]{1,0:T(8,128)(2,1)} %get-tuple-element.827, bf16[32,8192]{1,0:T(8,128)(2,1)S(1)} %get-tuple-element.763, bf16[8192,512]{1,0:T(8,128)(2,1)} %get-tuple-element.826, f32[8192]{0:T(1024)S(1)} %bitcast.141, f32[32]{0:T(128)S(1)} %add_rsqrt_fusion.4), kind=kOutput, calls=%fused_computation.1.clone.1 | convolution fusion | flops 538787840 | bytes 17858688 | tf_op jit(solution)/shard_map/while/body/eval_jaxpr/dot_general | solution.py:91
  299.9 8.9 %fusion.69 = bf16[32,8192]{1,0:T(8,128)(2,1)S(1)} fusion(bf16[512,8192]{1,0:T(8,128)(2,1)} %get-tuple-element.827, bf16[32,8192]{1,0:T(8,128)(2,1)S(1)} %get-tuple-element.763, bf16[8192,512]{1,0:T(8,128)(2,1)} %get-tuple-element.826, f32[8192]{0:T(1024)S(1)} %bitcast.141, f32[32]{0:T(128)S(1)} %add_rsqrt_fusion.4), kind=kOutput, calls=%fused_computation.1.clone.1 | convolution fusion | flops 538787840 | bytes 17858688 | tf_op jit(solution)/shard_map/while/body/eval_jaxpr/dot_general | solution.py:91
  311.9 340.2 %while.42 = (s32[]{:T(128)}, bf16[32,8192]{1,0:T(8,128)(2,1)}, bf16[6,32,8192]{2,1,0:T(8,128)(2,1)S(1)}, bf16[6,32,512]{2,1,0:T(8,128)(2,1)S(1)}, bf16[6,32,512]...) while((s32[]{:T(128)}, bf16[32,8192]{1,0:T(8,128)(2,1)}, ...), condition=%wide.region_6.7_spmd.clone, body=%wide.region_3.6_spmd.clone.sunk | while | flops 812908544 | bytes 98603504 | solution.py:138
  317.8 5.3 bitcast_dynamic-update-slice_fusion.9
  342.6 5.3 bitcast_dynamic-update-slice_fusion.9
  367.5 5.3 bitcast_dynamic-update-slice_fusion.9
  441.2 5.3 bitcast_dynamic-update-slice_fusion.9
  570.3 5.3 bitcast_dynamic-update-slice_fusion.9
  604.4 6.2 collective-permute-done.1
  634.2 6.6 collective-permute-done.1
  660.5 34.1 %all-to-all-start.1 = ((bf16[192,16,512]{2,0,1:T(8,128)(2,1)}), bf16[192,16,512]{2,0,1:T(8,128)(2,1)}, u32[]{:S(2)}, u32[]{:S(2)}) async-start(bf16[192,16,512]{2,0,1:T(8,128)(2,1)} %copy.9), calls=%async_computation.1 | async-start | bytes 6291456 | tf_op jit(solution)/shard_map/all_to_all | solution.py:149
  699.3 38.8 %all-to-all-done.1 = bf16[192,16,512]{2,0,1:T(8,128)(2,1)} async-done(((bf16[192,16,512]{2,0,1:T(8,128)(2,1)}), bf16[192,16,512]{2,0,1:T(8,128)(2,1)}, u32[]{:S(2)}, u32[]{:S(2)}) %all-to-all-start.1) | async-done | bytes 3145760 | tf_op jit(solution)/shard_map/all_to_all | solution.py:149
  738.1 11.5 %all-to-all-start = ((bf16[192,16,512]{2,0,1:T(8,128)(2,1)}), bf16[192,16,512]{2,0,1:T(8,128)(2,1)S(1)}, u32[]{:S(2)}, u32[]{:S(2)}) async-start(bf16[192,16,512]{2,0,1:T(8,128)(2,1)} %copy.8), calls=%async_computation | async-start | bytes 6291456 | tf_op jit(solution)/shard_map/all_to_all | solution.py:148
  749.6 43.6 %all-gather.2.cloned.1.call-done = bf16[3072,1024]{1,0:T(8,128)(2,1)} async-done(((bf16[192,1024]{1,0:T(8,128)(2,1)}), bf16[3072,1024]{1,0:T(8,128)(2,1)}) %all-gather.2.cloned.1.call-update) | async-done | bytes 6291472 | tf_op jit(solution)/shard_map/all_gather | solution.py:18
  798.1 7.6 convolution_convert_fusion
  805.7 7.6 convolution_convert_fusion.1
  813.3 5.5 reduce_sum.69
  818.8 5.5 reduce_sum.68
  (375 shorter events, 468.5 us)
Async XLA Ops:
  7.2 786.0 %all-gather.2.cloned.1.call-start = ((), (), s32[]{:S(2)}) async-start(), calls=%async_computation.2 | async-start | bytes 6684672 | tf_op jit(solution)/shard_map/all_gather | solution.py:18
  9.3 14.6 %collective-permute-start = (bf16[32,8192]{1,0:T(8,128)(2,1)S(1)}, bf16[32,8192]{1,0:T(8,128)(2,1)S(1)}, u32[]{:S(2)}, u32[]{:S(2)}) collective-permute-start(bf16[32,8192]{1,0:T(8,128)(2,1)S(1)} %broadcast_select_fusion.4), channel_id=1, source_target_pairs={{0,16},{16,32},{32,48},{48,64},{64,80},{80,96},{96,112},{1,17},{17... | collective-permute-start | bytes 1572872 | tf_op jit(solution)/shard_map/while/body/eval_jaxpr/ppermute | solution.py:12
  35.2 13.8 %collective-permute-start = (bf16[32,8192]{1,0:T(8,128)(2,1)S(1)}, bf16[32,8192]{1,0:T(8,128)(2,1)S(1)}, u32[]{:S(2)}, u32[]{:S(2)}) collective-permute-start(bf16[32,8192]{1,0:T(8,128)(2,1)S(1)} %broadcast_select_fusion.4), channel_id=1, source_target_pairs={{0,16},{16,32},{32,48},{48,64},{64,80},{80,96},{96,112},{1,17},{17... | collective-permute-start | bytes 1572872 | tf_op jit(solution)/shard_map/while/body/eval_jaxpr/ppermute | solution.py:12
  60.2 12.9 %collective-permute-start = (bf16[32,8192]{1,0:T(8,128)(2,1)S(1)}, bf16[32,8192]{1,0:T(8,128)(2,1)S(1)}, u32[]{:S(2)}, u32[]{:S(2)}) collective-permute-start(bf16[32,8192]{1,0:T(8,128)(2,1)S(1)} %broadcast_select_fusion.4), channel_id=1, source_target_pairs={{0,16},{16,32},{32,48},{48,64},{64,80},{80,96},{96,112},{1,17},{17... | collective-permute-start | bytes 1572872 | tf_op jit(solution)/shard_map/while/body/eval_jaxpr/ppermute | solution.py:12
  84.4 12.6 %collective-permute-start = (bf16[32,8192]{1,0:T(8,128)(2,1)S(1)}, bf16[32,8192]{1,0:T(8,128)(2,1)S(1)}, u32[]{:S(2)}, u32[]{:S(2)}) collective-permute-start(bf16[32,8192]{1,0:T(8,128)(2,1)S(1)} %broadcast_select_fusion.4), channel_id=1, source_target_pairs={{0,16},{16,32},{32,48},{48,64},{64,80},{80,96},{96,112},{1,17},{17... | collective-permute-start | bytes 1572872 | tf_op jit(solution)/shard_map/while/body/eval_jaxpr/ppermute | solution.py:12
  108.2 11.9 %collective-permute-start = (bf16[32,8192]{1,0:T(8,128)(2,1)S(1)}, bf16[32,8192]{1,0:T(8,128)(2,1)S(1)}, u32[]{:S(2)}, u32[]{:S(2)}) collective-permute-start(bf16[32,8192]{1,0:T(8,128)(2,1)S(1)} %broadcast_select_fusion.4), channel_id=1, source_target_pairs={{0,16},{16,32},{32,48},{48,64},{64,80},{80,96},{96,112},{1,17},{17... | collective-permute-start | bytes 1572872 | tf_op jit(solution)/shard_map/while/body/eval_jaxpr/ppermute | solution.py:12
  131.4 11.1 %collective-permute-start = (bf16[32,8192]{1,0:T(8,128)(2,1)S(1)}, bf16[32,8192]{1,0:T(8,128)(2,1)S(1)}, u32[]{:S(2)}, u32[]{:S(2)}) collective-permute-start(bf16[32,8192]{1,0:T(8,128)(2,1)S(1)} %broadcast_select_fusion.4), channel_id=1, source_target_pairs={{0,16},{16,32},{32,48},{48,64},{64,80},{80,96},{96,112},{1,17},{17... | collective-permute-start | bytes 1572872 | tf_op jit(solution)/shard_map/while/body/eval_jaxpr/ppermute | solution.py:12
  153.8 11.1 %collective-permute-start = (bf16[32,8192]{1,0:T(8,128)(2,1)S(1)}, bf16[32,8192]{1,0:T(8,128)(2,1)S(1)}, u32[]{:S(2)}, u32[]{:S(2)}) collective-permute-start(bf16[32,8192]{1,0:T(8,128)(2,1)S(1)} %broadcast_select_fusion.4), channel_id=1, source_target_pairs={{0,16},{16,32},{32,48},{48,64},{64,80},{80,96},{96,112},{1,17},{17... | collective-permute-start | bytes 1572872 | tf_op jit(solution)/shard_map/while/body/eval_jaxpr/ppermute | solution.py:12
  176.2 10.8 %collective-permute-start = (bf16[32,8192]{1,0:T(8,128)(2,1)S(1)}, bf16[32,8192]{1,0:T(8,128)(2,1)S(1)}, u32[]{:S(2)}, u32[]{:S(2)}) collective-permute-start(bf16[32,8192]{1,0:T(8,128)(2,1)S(1)} %broadcast_select_fusion.4), channel_id=1, source_target_pairs={{0,16},{16,32},{32,48},{48,64},{64,80},{80,96},{96,112},{1,17},{17... | collective-permute-start | bytes 1572872 | tf_op jit(solution)/shard_map/while/body/eval_jaxpr/ppermute | solution.py:12
  198.3 10.8 %collective-permute-start = (bf16[32,8192]{1,0:T(8,128)(2,1)S(1)}, bf16[32,8192]{1,0:T(8,128)(2,1)S(1)}, u32[]{:S(2)}, u32[]{:S(2)}) collective-permute-start(bf16[32,8192]{1,0:T(8,128)(2,1)S(1)} %broadcast_select_fusion.4), channel_id=1, source_target_pairs={{0,16},{16,32},{32,48},{48,64},{64,80},{80,96},{96,112},{1,17},{17... | collective-permute-start | bytes 1572872 | tf_op jit(solution)/shard_map/while/body/eval_jaxpr/ppermute | solution.py:12
  220.4 10.8 %collective-permute-start = (bf16[32,8192]{1,0:T(8,128)(2,1)S(1)}, bf16[32,8192]{1,0:T(8,128)(2,1)S(1)}, u32[]{:S(2)}, u32[]{:S(2)}) collective-permute-start(bf16[32,8192]{1,0:T(8,128)(2,1)S(1)} %broadcast_select_fusion.4), channel_id=1, source_target_pairs={{0,16},{16,32},{32,48},{48,64},{64,80},{80,96},{96,112},{1,17},{17... | collective-permute-start | bytes 1572872 | tf_op jit(solution)/shard_map/while/body/eval_jaxpr/ppermute | solution.py:12
  242.5 10.8 %collective-permute-start = (bf16[32,8192]{1,0:T(8,128)(2,1)S(1)}, bf16[32,8192]{1,0:T(8,128)(2,1)S(1)}, u32[]{:S(2)}, u32[]{:S(2)}) collective-permute-start(bf16[32,8192]{1,0:T(8,128)(2,1)S(1)} %broadcast_select_fusion.4), channel_id=1, source_target_pairs={{0,16},{16,32},{32,48},{48,64},{64,80},{80,96},{96,112},{1,17},{17... | collective-permute-start | bytes 1572872 | tf_op jit(solution)/shard_map/while/body/eval_jaxpr/ppermute | solution.py:12
  264.6 10.8 %collective-permute-start = (bf16[32,8192]{1,0:T(8,128)(2,1)S(1)}, bf16[32,8192]{1,0:T(8,128)(2,1)S(1)}, u32[]{:S(2)}, u32[]{:S(2)}) collective-permute-start(bf16[32,8192]{1,0:T(8,128)(2,1)S(1)} %broadcast_select_fusion.4), channel_id=1, source_target_pairs={{0,16},{16,32},{32,48},{48,64},{64,80},{80,96},{96,112},{1,17},{17... | collective-permute-start | bytes 1572872 | tf_op jit(solution)/shard_map/while/body/eval_jaxpr/ppermute | solution.py:12
  286.7 10.8 %collective-permute-start = (bf16[32,8192]{1,0:T(8,128)(2,1)S(1)}, bf16[32,8192]{1,0:T(8,128)(2,1)S(1)}, u32[]{:S(2)}, u32[]{:S(2)}) collective-permute-start(bf16[32,8192]{1,0:T(8,128)(2,1)S(1)} %broadcast_select_fusion.4), channel_id=1, source_target_pairs={{0,16},{16,32},{32,48},{48,64},{64,80},{80,96},{96,112},{1,17},{17... | collective-permute-start | bytes 1572872 | tf_op jit(solution)/shard_map/while/body/eval_jaxpr/ppermute | solution.py:12
  312.7 11.6 %collective-permute-start.1 = (bf16[32,8192]{1,0:T(8,128)(2,1)}, bf16[32,8192]{1,0:T(8,128)(2,1)}, u32[]{:S(2)}, u32[]{:S(2)}) collective-permute-start(bf16[32,8192]{1,0:T(8,128)(2,1)} %broadcast_select_fusion.5), channel_id=1, source_target_pairs={{16,0},{32,16},{48,32},{64,48},{80,64},{96,80},{112,96},{17,1},{33... | collective-permute-start | bytes 1572872 | tf_op jit(solution)/shard_map/while/body/eval_jaxpr/ppermute | solution.py:12
  337.5 11.8 %collective-permute-start.1 = (bf16[32,8192]{1,0:T(8,128)(2,1)}, bf16[32,8192]{1,0:T(8,128)(2,1)}, u32[]{:S(2)}, u32[]{:S(2)}) collective-permute-start(bf16[32,8192]{1,0:T(8,128)(2,1)} %broadcast_select_fusion.5), channel_id=1, source_target_pairs={{16,0},{32,16},{48,32},{64,48},{80,64},{96,80},{112,96},{17,1},{33... | collective-permute-start | bytes 1572872 | tf_op jit(solution)/shard_map/while/body/eval_jaxpr/ppermute | solution.py:12
  362.5 11.4 %collective-permute-start.1 = (bf16[32,8192]{1,0:T(8,128)(2,1)}, bf16[32,8192]{1,0:T(8,128)(2,1)}, u32[]{:S(2)}, u32[]{:S(2)}) collective-permute-start(bf16[32,8192]{1,0:T(8,128)(2,1)} %broadcast_select_fusion.5), channel_id=1, source_target_pairs={{16,0},{32,16},{48,32},{64,48},{80,64},{96,80},{112,96},{17,1},{33... | collective-permute-start | bytes 1572872 | tf_op jit(solution)/shard_map/while/body/eval_jaxpr/ppermute | solution.py:12
  387.0 11.4 %collective-permute-start.1 = (bf16[32,8192]{1,0:T(8,128)(2,1)}, bf16[32,8192]{1,0:T(8,128)(2,1)}, u32[]{:S(2)}, u32[]{:S(2)}) collective-permute-start(bf16[32,8192]{1,0:T(8,128)(2,1)} %broadcast_select_fusion.5), channel_id=1, source_target_pairs={{16,0},{32,16},{48,32},{64,48},{80,64},{96,80},{112,96},{17,1},{33... | collective-permute-start | bytes 1572872 | tf_op jit(solution)/shard_map/while/body/eval_jaxpr/ppermute | solution.py:12
  411.6 11.4 %collective-permute-start.1 = (bf16[32,8192]{1,0:T(8,128)(2,1)}, bf16[32,8192]{1,0:T(8,128)(2,1)}, u32[]{:S(2)}, u32[]{:S(2)}) collective-permute-start(bf16[32,8192]{1,0:T(8,128)(2,1)} %broadcast_select_fusion.5), channel_id=1, source_target_pairs={{16,0},{32,16},{48,32},{64,48},{80,64},{96,80},{112,96},{17,1},{33... | collective-permute-start | bytes 1572872 | tf_op jit(solution)/shard_map/while/body/eval_jaxpr/ppermute | solution.py:12
  436.1 11.4 %collective-permute-start.1 = (bf16[32,8192]{1,0:T(8,128)(2,1)}, bf16[32,8192]{1,0:T(8,128)(2,1)}, u32[]{:S(2)}, u32[]{:S(2)}) collective-permute-start(bf16[32,8192]{1,0:T(8,128)(2,1)} %broadcast_select_fusion.5), channel_id=1, source_target_pairs={{16,0},{32,16},{48,32},{64,48},{80,64},{96,80},{112,96},{17,1},{33... | collective-permute-start | bytes 1572872 | tf_op jit(solution)/shard_map/while/body/eval_jaxpr/ppermute | solution.py:12
  460.7 11.4 %collective-permute-start.1 = (bf16[32,8192]{1,0:T(8,128)(2,1)}, bf16[32,8192]{1,0:T(8,128)(2,1)}, u32[]{:S(2)}, u32[]{:S(2)}) collective-permute-start(bf16[32,8192]{1,0:T(8,128)(2,1)} %broadcast_select_fusion.5), channel_id=1, source_target_pairs={{16,0},{32,16},{48,32},{64,48},{80,64},{96,80},{112,96},{17,1},{33... | collective-permute-start | bytes 1572872 | tf_op jit(solution)/shard_map/while/body/eval_jaxpr/ppermute | solution.py:12
  485.3 12.6 %collective-permute-start.1 = (bf16[32,8192]{1,0:T(8,128)(2,1)}, bf16[32,8192]{1,0:T(8,128)(2,1)}, u32[]{:S(2)}, u32[]{:S(2)}) collective-permute-start(bf16[32,8192]{1,0:T(8,128)(2,1)} %broadcast_select_fusion.5), channel_id=1, source_target_pairs={{16,0},{32,16},{48,32},{64,48},{80,64},{96,80},{112,96},{17,1},{33... | collective-permute-start | bytes 1572872 | tf_op jit(solution)/shard_map/while/body/eval_jaxpr/ppermute | solution.py:12
  511.1 13.4 %collective-permute-start.1 = (bf16[32,8192]{1,0:T(8,128)(2,1)}, bf16[32,8192]{1,0:T(8,128)(2,1)}, u32[]{:S(2)}, u32[]{:S(2)}) collective-permute-start(bf16[32,8192]{1,0:T(8,128)(2,1)} %broadcast_select_fusion.5), channel_id=1, source_target_pairs={{16,0},{32,16},{48,32},{64,48},{80,64},{96,80},{112,96},{17,1},{33... | collective-permute-start | bytes 1572872 | tf_op jit(solution)/shard_map/while/body/eval_jaxpr/ppermute | solution.py:12
  537.6 14.5 %collective-permute-start.1 = (bf16[32,8192]{1,0:T(8,128)(2,1)}, bf16[32,8192]{1,0:T(8,128)(2,1)}, u32[]{:S(2)}, u32[]{:S(2)}) collective-permute-start(bf16[32,8192]{1,0:T(8,128)(2,1)} %broadcast_select_fusion.5), channel_id=1, source_target_pairs={{16,0},{32,16},{48,32},{64,48},{80,64},{96,80},{112,96},{17,1},{33... | collective-permute-start | bytes 1572872 | tf_op jit(solution)/shard_map/while/body/eval_jaxpr/ppermute | solution.py:12
  565.2 15.5 %collective-permute-start.1 = (bf16[32,8192]{1,0:T(8,128)(2,1)}, bf16[32,8192]{1,0:T(8,128)(2,1)}, u32[]{:S(2)}, u32[]{:S(2)}) collective-permute-start(bf16[32,8192]{1,0:T(8,128)(2,1)} %broadcast_select_fusion.5), channel_id=1, source_target_pairs={{16,0},{32,16},{48,32},{64,48},{80,64},{96,80},{112,96},{17,1},{33... | collective-permute-start | bytes 1572872 | tf_op jit(solution)/shard_map/while/body/eval_jaxpr/ppermute | solution.py:12
  568.6 17.7 %slice-start = ((s8[8388608]{0:T(1024)(128)(4,1)}), s8[4194304]{0:T(1024)(128)(4,1)S(1)}, s32[]{:S(2)}) async-start(s8[8388608]{0:T(1024)(128)(4,1)} %bitcast.136), calls=%async_computation.3 | async-start | bytes 8388608 | tf_op jit(solution)/shard_map/while
  594.0 16.6 %collective-permute-start.1 = (bf16[32,8192]{1,0:T(8,128)(2,1)}, bf16[32,8192]{1,0:T(8,128)(2,1)}, u32[]{:S(2)}, u32[]{:S(2)}) collective-permute-start(bf16[32,8192]{1,0:T(8,128)(2,1)} %broadcast_select_fusion.5), channel_id=1, source_target_pairs={{16,0},{32,16},{48,32},{64,48},{80,64},{96,80},{112,96},{17,1},{33... | collective-permute-start | bytes 1572872 | tf_op jit(solution)/shard_map/while/body/eval_jaxpr/ppermute | solution.py:12
  597.3 18.7 %slice-start = ((s8[8388608]{0:T(1024)(128)(4,1)}), s8[4194304]{0:T(1024)(128)(4,1)S(1)}, s32[]{:S(2)}) async-start(s8[8388608]{0:T(1024)(128)(4,1)} %bitcast.136), calls=%async_computation.3 | async-start | bytes 8388608 | tf_op jit(solution)/shard_map/while
  623.8 17.0 %collective-permute-start.1 = (bf16[32,8192]{1,0:T(8,128)(2,1)}, bf16[32,8192]{1,0:T(8,128)(2,1)}, u32[]{:S(2)}, u32[]{:S(2)}) collective-permute-start(bf16[32,8192]{1,0:T(8,128)(2,1)} %broadcast_select_fusion.5), channel_id=1, source_target_pairs={{16,0},{32,16},{48,32},{64,48},{80,64},{96,80},{112,96},{17,1},{33... | collective-permute-start | bytes 1572872 | tf_op jit(solution)/shard_map/while/body/eval_jaxpr/ppermute | solution.py:12
  627.1 19.1 %slice-start = ((s8[8388608]{0:T(1024)(128)(4,1)}), s8[4194304]{0:T(1024)(128)(4,1)S(1)}, s32[]{:S(2)}) async-start(s8[8388608]{0:T(1024)(128)(4,1)} %bitcast.136), calls=%async_computation.3 | async-start | bytes 8388608 | tf_op jit(solution)/shard_map/while
  660.5 77.6 %all-to-all-start.1 = ((bf16[192,16,512]{2,0,1:T(8,128)(2,1)}), bf16[192,16,512]{2,0,1:T(8,128)(2,1)}, u32[]{:S(2)}, u32[]{:S(2)}) async-start(bf16[192,16,512]{2,0,1:T(8,128)(2,1)} %copy.9), calls=%async_computation.1 | async-start | bytes 6291456 | tf_op jit(solution)/shard_map/all_to_all | solution.py:149
  738.1 67.6 %all-to-all-start = ((bf16[192,16,512]{2,0,1:T(8,128)(2,1)}), bf16[192,16,512]{2,0,1:T(8,128)(2,1)S(1)}, u32[]{:S(2)}, u32[]{:S(2)}) async-start(bf16[192,16,512]{2,0,1:T(8,128)(2,1)} %copy.8), calls=%async_computation | async-start | bytes 6291456 | tf_op jit(solution)/shard_map/all_to_all | solution.py:148
  (38 other events, 453.9 us)
Sparse Core Ops, SparseCore 0:
  654.0 139.1 all-gather.1
where the time goes:
time: 839 us; the launch traced here: 831 us
  matrix products  290 us (35%)
  waiting for transfers between devices  163 us (19%)
  other arithmetic  162 us (19%)
  starting transfers between devices  123 us (15%)
  local copies, waits for them, and re-layouts  53.5 us (6%)
  loops' own time  26 us (3%)
  between operations  14.1 us (2%)
    dot_general x13, matrix products, forward_tick(): jnp.dot(hidden, weight_second, preferred_element_type=jnp.float32)  116 us
    ppermute x26, waiting for transfers between devices, passed_along(): return lax.ppermute(value, axis, pairs)  80.5 us
    dynamic_update_slice x39, other arithmetic, put_slot(): lax.dynamic_update_index_in_dim(buffer, jnp.where(active_flag, new_value,...  77.4 us
    ppermute x26, starting transfers between devices, passed_along(): return lax.ppermute(value, axis, pairs)  77.3 us
    dot_general x13, matrix products, inner_section(): pre_act = jnp.dot(normed, weight_first, preferred_element_type=jnp.float32)  69.1 us
    dot_general x13, matrix products, backward_section(): jnp.einsum('tr,dr->td', grad_pre, weight_first, preferred_element_type=jn...  48 us
    all_gather x1, waiting for transfers between devices, sent_together(): result = lax.all_gather(both, axis, axis=dim, tiled=True)  43.6 us
    dot_general x13, matrix products, backward_section(): jnp.einsum('td,rd->tr', incoming_gradient, weight_second, preferred_eleme...  41.7 us
  transfers between devices with their start and end apart: 29, of which 28 were waited for; matrix products, arithmetic and copies ran while one was open for 20% of the time, Pallas kernels for 0%

commit v1 on v0

v1 whole, which is shorter than its diff:
```python
import functools

import jax
import jax.numpy as jnp
from jax import lax
from jax.experimental import pallas as pl
from jax.experimental.pallas import tpu as pltpu
from jax.sharding import PartitionSpec as P

EPSILON = 1e-05
SPLIT = 2
SKEW = 2
AUX = 128
CUT = 1024

F32 = jnp.float32
BF16 = jnp.bfloat16


def hbm():
    return pl.BlockSpec(memory_space=pl.ANY)


def vmem():
    return pl.BlockSpec(memory_space=pltpu.VMEM)


def smem():
    return pl.BlockSpec(memory_space=pltpu.SMEM)


def load_kernel(*refs):
    count = (len(refs) - 1) // 2
    sems = refs[-1]
    copies = [
        pltpu.make_async_copy(refs[k], refs[count + k], sems.at[k]) for k in range(count)
    ]
    for copy in copies:
        copy.start()
    for copy in copies:
        copy.wait()


def resident(*arrays):
    return pl.pallas_call(
        load_kernel,
        out_shape=tuple(pltpu.VMEM(a.shape, a.dtype) for a in arrays),
        in_specs=[hbm()] * len(arrays),
        out_specs=tuple(vmem() for a in arrays),
        scratch_shapes=[pltpu.SemaphoreType.DMA((len(arrays),))],
        compiler_params=pltpu.CompilerParams(vmem_limit_bytes=1 << 20),
        name="resident",
    )(*arrays)


def fetch(take, source, other, target, sem):
    @pl.when(take)
    def _():
        copy = pltpu.make_async_copy(source, target, sem)
        copy.start()
        copy.wait()

    @pl.when(jnp.logical_not(take))
    def _():
        copy = pltpu.make_async_copy(other, target, sem)
        copy.start()
        copy.wait()


def forward_kernel(chunk, slot, meta, plan, arrived, inputs, gain, w_in, w_out, *rest):
    if slot > 0:
        rest = rest[3:]
    send, normed_all, aux_all, hidden_all, x, normed, aux, hidden, sems = rest
    rows, width = x.shape
    inner = w_in.shape[1]
    if chunk is None:
        copy = pltpu.make_async_copy(arrived, x, sems.at[0])
        copy.start()
        copy.wait()
    else:
        block, part = divmod(chunk, SPLIT)
        fresh = inputs.at[plan[block], pl.ds(part * rows, rows), :]
        fetch(meta[0] == 0, fresh, arrived, x, sems.at[0])
    total = jnp.zeros((rows, CUT), F32)
    for j in range(width // CUT):
        value = x[:, j * CUT : (j + 1) * CUT].astype(F32)
        total = total + value * value
    inverse = lax.rsqrt(jnp.sum(total, axis=1, keepdims=True) / width + EPSILON)
    pre = jnp.zeros((rows, inner), F32)
    for j in range(width // CUT):
        cols = slice(j * CUT, (j + 1) * CUT)
        piece = (x[:, cols].astype(F32) * inverse * gain[:, cols]).astype(BF16)
        normed[:, cols] = piece
        pre = pre + jnp.dot(piece, w_in[cols, :], preferred_element_type=F32)
    at = pl.ds(slot * rows, rows)
    first = pltpu.make_async_copy(normed, normed_all.at[at, :], sems.at[1])
    first.start()
    aux[:, :inner] = pre
    aux[:, inner:] = jnp.broadcast_to(inverse, (rows, AUX))
    second = pltpu.make_async_copy(aux, aux_all.at[at, :], sems.at[2])
    second.start()
    act = (pre / (1.0 + jnp.exp(-pre))).astype(BF16)
    hidden[...] = act
    third = pltpu.make_async_copy(hidden, hidden_all.at[at, :], sems.at[3])
    third.start()
    for j in range(width // CUT):
        cols = slice(j * CUT, (j + 1) * CUT)
        delta = jnp.dot(act, w_out[:, cols], preferred_element_type=F32)
        send[:, cols] = (x[:, cols].astype(F32) + delta).astype(BF16)
    first.wait()
    second.wait()
    third.wait()


def forward_step(slot, ticks, chunks, rows, meta, plan, arrived, inputs, gain, w_in, w_out, kept):
    width, inner = w_in.shape
    chunk = slot if slot < chunks else None
    shapes = (
        jax.ShapeDtypeStruct((rows, width), BF16),
        jax.ShapeDtypeStruct((ticks * rows, width), BF16),
        jax.ShapeDtypeStruct((ticks * rows, inner + AUX), F32),
        jax.ShapeDtypeStruct((ticks * rows, inner), BF16),
    )
    specs = [smem(), smem(), hbm(), hbm(), vmem(), vmem(), vmem()] + [hbm()] * len(kept)
    return pl.pallas_call(
        functools.partial(forward_kernel, chunk, slot),
        out_shape=shapes,
        in_specs=specs,
        out_specs=(vmem(), hbm(), hbm(), hbm()),
        scratch_shapes=[
            pltpu.VMEM((rows, width), BF16),
            pltpu.VMEM((rows, width), BF16),
            pltpu.VMEM((rows, inner + AUX), F32),
            pltpu.VMEM((rows, inner), BF16),
            pltpu.SemaphoreType.DMA((4,)),
        ],
        input_output_aliases={7 + k: 1 + k for k in range(len(kept))},
        compiler_params=pltpu.CompilerParams(vmem_limit_bytes=8 << 20),
        cost_estimate=pl.CostEstimate(
            flops=4 * rows * width * inner, bytes_accessed=10 << 20, transcendentals=0
        ),
        name="forward_step",
    )(meta, plan, arrived, inputs, gain, w_in, w_out, *kept)


NT = (((1,), (1,)), ((), ()))


def backward_kernel(
    chunk, slot, meta, arrived, cotangent, normed_all, aux_all, gain, w_in, w_out, *rest
):
    if slot > 0:
        rest = rest[2:]
    send, up_all, grad_all, up, normed, aux, grad, sems = rest
    rows, width = up.shape
    inner = w_in.shape[1]
    source = pl.ds(pl.multiple_of(meta[1] * rows, rows), rows)
    load_normed = pltpu.make_async_copy(normed_all.at[source, :], normed, sems.at[1])
    load_normed.start()
    load_aux = pltpu.make_async_copy(aux_all.at[source, :], aux, sems.at[2])
    load_aux.start()
    if chunk is None:
        copy = pltpu.make_async_copy(arrived, up, sems.at[0])
        copy.start()
        copy.wait()
    else:
        block, part = divmod(chunk, SPLIT)
        fresh = cotangent.at[block, pl.ds(part * rows, rows), :]
        fetch(meta[0] == 1, fresh, arrived, up, sems.at[0])
    at = pl.ds(slot * rows, rows)
    store_up = pltpu.make_async_copy(up, up_all.at[at, :], sems.at[3])
    store_up.start()
    grad_hidden = jnp.zeros((rows, inner), F32)
    for j in range(width // CUT):
        cols = slice(j * CUT, (j + 1) * CUT)
        grad_hidden = grad_hidden + lax.dot_general(
            up[:, cols], w_out[:, cols], NT, preferred_element_type=F32
        )
    load_aux.wait()
    pre = aux[:, :inner]
    inverse = aux[:, inner : inner + 1]
    gate = 1.0 / (1.0 + jnp.exp(-pre))
    grad_pre = (grad_hidden * gate * (1.0 + pre * (1.0 - gate))).astype(BF16)
    grad[...] = grad_pre
    store_grad = pltpu.make_async_copy(grad, grad_all.at[at, :], sems.at[4])
    store_grad.start()
    mean = jnp.sum(grad_pre.astype(F32) * pre, axis=1, keepdims=True) / width
    load_normed.wait()
    for j in range(width // CUT):
        cols = slice(j * CUT, (j + 1) * CUT)
        back = lax.dot_general(grad_pre, w_in[cols, :], NT, preferred_element_type=F32)
        scale = gain[:, cols]
        xhat = normed[:, cols].astype(F32) * (1.0 / scale)
        send[:, cols] = (
            up[:, cols].astype(F32) + inverse * (back * scale - xhat * mean)
        ).astype(BF16)
    store_up.wait()
    store_grad.wait()


def backward_step(
    slot, ticks, chunks, rows, meta, arrived, cotangent, normed_all, aux_all, gain, w_in, w_out, kept
):
    width, inner = w_in.shape
    chunk = slot if slot < chunks else None
    shapes = (
        jax.ShapeDtypeStruct((rows, width), BF16),
        jax.ShapeDtypeStruct((ticks * rows, width), BF16),
        jax.ShapeDtypeStruct((ticks * rows, inner), BF16),
    )
    specs = [smem()] + [hbm()] * 4 + [vmem()] * 3 + [hbm()] * len(kept)
    return pl.pallas_call(
        functools.partial(backward_kernel, chunk, slot),
        out_shape=shapes,
        in_specs=specs,
        out_specs=(vmem(), hbm(), hbm()),
        scratch_shapes=[
            pltpu.VMEM((rows, width), BF16),
            pltpu.VMEM((rows, width), BF16),
            pltpu.VMEM((rows, inner + AUX), F32),
            pltpu.VMEM((rows, inner), BF16),
            pltpu.SemaphoreType.DMA((5,)),
        ],
        input_output_aliases={8 + k: 1 + k for k in range(len(kept))},
        compiler_params=pltpu.CompilerParams(vmem_limit_bytes=8 << 20),
        cost_estimate=pl.CostEstimate(
            flops=4 * rows * width * inner, bytes_accessed=10 << 20, transcendentals=0
        ),
        name="backward_step",
    )(meta, arrived, cotangent, normed_all, aux_all, gain, w_in, w_out, *kept)


def gathered(array, axis):
    return lax.all_gather(array, axis, axis=0, tiled=True)


def columns(array, axis):
    return lax.all_to_all(array, axis, split_axis=1, concat_axis=0, tiled=True)


def contracted(left, right):
    return lax.dot_general(left, right, (((0,), (0,)), ((), ())), preferred_element_type=F32)


def per_device(inputs, cotangent, plan_order, norm_gain, weight_in, weight_out):
    sections = lax.axis_size("pipe")
    section = lax.axis_index("pipe")
    micro_count, row_count, width = inputs.shape
    rows = row_count // SPLIT
    chunks = micro_count * SPLIT
    last = SKEW * (sections - 1)
    ticks = chunks + last

    def held(tick):
        return [s for s in range(sections) if 0 <= tick - SKEW * s < chunks]

    w_in, w_out = resident(weight_in[0], weight_out[0])
    empty = jnp.zeros((rows, width), BF16)
    plan = plan_order.astype(jnp.int32)

    meta = jnp.stack([section, section]).astype(jnp.int32)
    moving = {}
    kept = ()
    for tick in range(ticks):
        arrived = moving.pop(tick, empty)
        send, *kept = forward_step(
            tick, ticks, chunks, rows, meta, plan, arrived, inputs, norm_gain, w_in, w_out, kept
        )
        pairs = [(s, s + 1) for s in held(tick) if s + 1 < sections]
        if pairs:
            moving[tick + SKEW] = lax.ppermute(send, "pipe", pairs)
    normed_all, aux_all, hidden_all = kept
    tokens = chunks * rows
    half = tokens // 2
    begin = section * (SKEW * rows)
    normed_own = lax.dynamic_slice(normed_all, (begin, 0), (tokens, width))
    hidden_own = lax.dynamic_slice(hidden_all, (begin, 0), (tokens, hidden_all.shape[1]))
    normed_cols = columns(normed_own, "dp")
    hidden_rows = gathered(hidden_own, "dp")

    moving = {}
    kept = ()
    is_last = (section == sections - 1).astype(jnp.int32)
    for tick in range(ticks):
        arrived = moving.pop(tick, empty)
        source = jnp.clip(tick - last + 2 * SKEW * section, 0, ticks - 1).astype(jnp.int32)
        send, *kept = backward_step(
            tick,
            ticks,
            chunks,
            rows,
            jnp.stack([is_last, source]),
            arrived,
            cotangent,
            normed_all,
            aux_all,
            norm_gain,
            w_in,
            w_out,
            kept,
        )
        pairs = [
            (sections - 1 - s, sections - 2 - s) for s in held(tick) if s + 1 < sections
        ]
        if pairs:
            moving[tick + SKEW] = lax.ppermute(send, "pipe", pairs)
    up_all, grad_all = kept
    begin = (sections - 1 - section) * (SKEW * rows)
    up_own = lax.dynamic_slice(up_all, (begin, 0), (tokens, width))
    grad_own = lax.dynamic_slice(grad_all, (begin, 0), (tokens, grad_all.shape[1]))
    up_cols = columns(up_own, "dp")
    grad_rows = gathered(grad_own, "dp")
    total_in = contracted(normed_cols, grad_rows).astype(BF16)
    total_out = contracted(hidden_rows, up_cols).astype(BF16)
    return total_in[None], total_out[None]


def solution(mesh):
    in_specs = (
        P(None, "dp", None),
        P(None, "dp", None),
        P(),
        P("pipe", None),
        P("pipe", None, None),
        P("pipe", None, None),
    )
    out_specs = (P("pipe", "dp", None), P("pipe", None, "dp"))
    return jax.shard_map(
        per_device, mesh=mesh, in_specs=in_specs, out_specs=out_specs, check_vma=False
    )
```

time: 839 us -> 908 us (1.082); the launches traced: 831 us -> 891 us
  matrix products: 290 us -> 10.9 us
  local copies, waits for them, and re-layouts: 53.5 us -> 313 us
  Pallas kernels: 0 us -> 230 us
  other arithmetic: 162 us -> 1.96 us
  starting transfers between devices: 123 us -> 236 us
  waiting for transfers between devices: 163 us -> 83.7 us
  loops' own time: 26 us -> 0 us
    unnamed x6 -> x234, local copies, waits for them, and re-layouts: 4.56 us -> 305 us
    dot_general x54 -> x2, matrix products: 290 us -> 10.9 us  [contracted(): lax.dot_general(left, right, (((0,), (0,)), ((), ())), preferred_element_...]
    pallas_call x0 -> x53, Pallas kernels: none -> 230 us  [the longest x26 143 us: backward_step(): pl.pallas_call(functools.partial(backward_kernel, chunk, slot), out_shape...]
    ppermute x26 -> x48, starting transfers between devices: 77.3 us -> 218 us  [per_device(): moving[tick + SKEW] = lax.ppermute(send, 'pipe', pairs)]
    dynamic_update_slice x39 -> x0, other arithmetic: 77.4 us -> none  [put_slot(): lax.dynamic_update_index_in_dim(buffer, jnp.where(active_flag, new_value,...]
    ppermute x26 -> x48, waiting for transfers between devices: 80.5 us -> 3.33 us  [per_device(): moving[tick + SKEW] = lax.ppermute(send, 'pipe', pairs)]
    all_gather x1 -> x2, waiting for transfers between devices: 43.6 us -> 0.01 us  [gathered(): return lax.all_gather(array, axis, axis=0, tiled=True)]
    all_to_all x2, waiting for transfers between devices: 38.8 us -> 80.3 us  [columns(): return lax.all_to_all(array, axis, split_axis=1, concat_axis=0, tiled=True)]
  transfers between devices with their start and end apart: 29 -> 52, of which waited for: 28 -> 6; matrix products, arithmetic and copies ran while one was open for 20% -> 2% of each run, Pallas kernels for 0% -> 25%
where the time goes in v1:
time: 908 us; the launch traced here: 891 us
  local copies, waits for them, and re-layouts  313 us (34%)
  starting transfers between devices  236 us (26%)
  Pallas kernels  230 us (25%)
  waiting for transfers between devices  83.7 us (9%)
  between operations  16 us (2%)
  matrix products  10.9 us (1%)
    unnamed x234, local copies, waits for them, and re-layouts  305 us
    ppermute x48, starting transfers between devices, per_device(): moving[tick + SKEW] = lax.ppermute(send, 'pipe', pairs)  218 us
    pallas_call x26, Pallas kernels, backward_step(): pl.pallas_call(functools.partial(backward_kernel, chunk, slot), out_shape...  143 us
    pallas_call x26, Pallas kernels, forward_step(): pl.pallas_call(functools.partial(forward_kernel, chunk, slot), out_shape=...  85.8 us
    all_to_all x2, waiting for transfers between devices, columns(): return lax.all_to_all(array, axis, split_axis=1, concat_axis=0, tiled=True)  80.3 us
  transfers between devices with their start and end apart: 52, of which 6 were waited for; matrix products, arithmetic and copies ran while one was open for 2% of the time, Pallas kernels for 25%

profile of v1, /device:TPU:1, one launch (start us, length us, event | category | flops | bytes accessed | tf_op | source)
XLA Modules:
  0.0 890.9 jit_solution(1821911442772699824)
XLA Ops:
  79.5 15.7 %collective-permute-start.11 = (bf16[16,8192]{1,0:T(8,128)(2,1)S(1)}, bf16[16,8192]{1,0:T(8,128)(2,1)S(1)}, u32[]{:S(2)}, u32[]{:S(2)}) collective-permute-start(bf16[16,8192]{1,0:T(8,128)(2,1)S(1)} %get-tuple-element.228), channel_id=1, source_target_pairs={{0,16},{16,32},{32,48},{48,64},{64,80},{80,96},{1,17},{17,33},{33,... | collective-permute-start | bytes 786440 | tf_op jit(solution)/shard_map/ppermute | solution.py:271
  98.4 10.2 %collective-permute-start.10 = (bf16[16,8192]{1,0:T(8,128)(2,1)S(1)}, bf16[16,8192]{1,0:T(8,128)(2,1)S(1)}, u32[]{:S(2)}, u32[]{:S(2)}) collective-permute-start(bf16[16,8192]{1,0:T(8,128)(2,1)S(1)} %get-tuple-element.227), channel_id=1, source_target_pairs={{0,16},{16,32},{32,48},{48,64},{64,80},{80,96},{1,17},{17,33},{33,... | collective-permute-start | bytes 786440 | tf_op jit(solution)/shard_map/ppermute | solution.py:271
  111.8 9.5 %collective-permute-start.13 = (bf16[16,8192]{1,0:T(8,128)(2,1)S(1)}, bf16[16,8192]{1,0:T(8,128)(2,1)S(1)}, u32[]{:S(2)}, u32[]{:S(2)}) collective-permute-start(bf16[16,8192]{1,0:T(8,128)(2,1)S(1)} %get-tuple-element.236), channel_id=1, source_target_pairs={{16,32},{32,48},{48,64},{64,80},{80,96},{96,112},{17,33},{33,49},{... | collective-permute-start | bytes 786440 | tf_op jit(solution)/shard_map/ppermute | solution.py:271
  124.6 10.2 %collective-permute-start.12 = (bf16[16,8192]{1,0:T(8,128)(2,1)S(1)}, bf16[16,8192]{1,0:T(8,128)(2,1)S(1)}, u32[]{:S(2)}, u32[]{:S(2)}) collective-permute-start(bf16[16,8192]{1,0:T(8,128)(2,1)S(1)} %get-tuple-element.235), channel_id=1, source_target_pairs={{16,32},{32,48},{48,64},{64,80},{80,96},{96,112},{17,33},{33,49},{... | collective-permute-start | bytes 786440 | tf_op jit(solution)/shard_map/ppermute | solution.py:271
  138.1 10.6 %collective-permute-start.15 = (bf16[16,8192]{1,0:T(8,128)(2,1)S(1)}, bf16[16,8192]{1,0:T(8,128)(2,1)S(1)}, u32[]{:S(2)}, u32[]{:S(2)}) collective-permute-start(bf16[16,8192]{1,0:T(8,128)(2,1)S(1)} %get-tuple-element.244), channel_id=1, source_target_pairs={{32,48},{48,64},{64,80},{80,96},{96,112},{33,49},{49,65},{65,81},{... | collective-permute-start | bytes 786440 | tf_op jit(solution)/shard_map/ppermute | solution.py:271
  151.9 10.2 %collective-permute-start.14 = (bf16[16,8192]{1,0:T(8,128)(2,1)S(1)}, bf16[16,8192]{1,0:T(8,128)(2,1)S(1)}, u32[]{:S(2)}, u32[]{:S(2)}) collective-permute-start(bf16[16,8192]{1,0:T(8,128)(2,1)S(1)} %get-tuple-element.243), channel_id=1, source_target_pairs={{32,48},{48,64},{64,80},{80,96},{96,112},{33,49},{49,65},{65,81},{... | collective-permute-start | bytes 786440 | tf_op jit(solution)/shard_map/ppermute | solution.py:271
  231.4 5.4 backward_step.26
  237.5 5.4 backward_step.27
  261.2 5.8 backward_step.28
  280.2 5.4 backward_step.29
  303.9 5.4 backward_step.30
  319.7 5.4 backward_step.31
  343.3 5.6 backward_step.32
  359.3 5.4 backward_step.33
  382.8 5.4 backward_step.34
  388.3 40.3 %collective-permute-start.33 = (bf16[16,8192]{1,0:T(8,128)(2,1)S(1)}, bf16[16,8192]{1,0:T(8,128)(2,1)S(1)}, u32[]{:S(2)}, u32[]{:S(2)}) collective-permute-start(bf16[16,8192]{1,0:T(8,128)(2,1)S(1)} %get-tuple-element.312), channel_id=1, source_target_pairs={{112,96},{96,80},{80,64},{64,48},{48,32},{113,97},{97,81},{81,65},... | collective-permute-start | bytes 786440 | tf_op jit(solution)/shard_map/ppermute | solution.py:306
  438.3 5.4 backward_step.35
  446.4 10.2 %collective-permute-start.32 = (bf16[16,8192]{1,0:T(8,128)(2,1)S(1)}, bf16[16,8192]{1,0:T(8,128)(2,1)S(1)}, u32[]{:S(2)}, u32[]{:S(2)}) collective-permute-start(bf16[16,8192]{1,0:T(8,128)(2,1)S(1)} %get-tuple-element.311), channel_id=1, source_target_pairs={{112,96},{96,80},{80,64},{64,48},{48,32},{113,97},{97,81},{81,65},... | collective-permute-start | bytes 786440 | tf_op jit(solution)/shard_map/ppermute | solution.py:306
  471.3 5.6 backward_step.36
  476.9 10.2 %collective-permute-start.35 = (bf16[16,8192]{1,0:T(8,128)(2,1)S(1)}, bf16[16,8192]{1,0:T(8,128)(2,1)S(1)}, u32[]{:S(2)}, u32[]{:S(2)}) collective-permute-start(bf16[16,8192]{1,0:T(8,128)(2,1)S(1)} %get-tuple-element.318), channel_id=1, source_target_pairs={{112,96},{96,80},{80,64},{64,48},{48,32},{32,16},{113,97},{97,81},... | collective-permute-start | bytes 786440 | tf_op jit(solution)/shard_map/ppermute | solution.py:306
  505.0 10.2 %collective-permute-start.34 = (bf16[16,8192]{1,0:T(8,128)(2,1)S(1)}, bf16[16,8192]{1,0:T(8,128)(2,1)S(1)}, u32[]{:S(2)}, u32[]{:S(2)}) collective-permute-start(bf16[16,8192]{1,0:T(8,128)(2,1)S(1)} %get-tuple-element.317), channel_id=1, source_target_pairs={{112,96},{96,80},{80,64},{64,48},{48,32},{32,16},{113,97},{97,81},... | collective-permute-start | bytes 786440 | tf_op jit(solution)/shard_map/ppermute | solution.py:306
  535.3 10.2 %collective-permute-start.37 = (bf16[16,8192]{1,0:T(8,128)(2,1)S(1)}, bf16[16,8192]{1,0:T(8,128)(2,1)S(1)}, u32[]{:S(2)}, u32[]{:S(2)}) collective-permute-start(bf16[16,8192]{1,0:T(8,128)(2,1)S(1)} %get-tuple-element.324), channel_id=1, source_target_pairs={{96,80},{80,64},{64,48},{48,32},{32,16},{16,0},{97,81},{81,65},{65... | collective-permute-start | bytes 786440 | tf_op jit(solution)/shard_map/ppermute | solution.py:306
  563.3 10.6 %collective-permute-start.36 = (bf16[16,8192]{1,0:T(8,128)(2,1)S(1)}, bf16[16,8192]{1,0:T(8,128)(2,1)S(1)}, u32[]{:S(2)}, u32[]{:S(2)}) collective-permute-start(bf16[16,8192]{1,0:T(8,128)(2,1)S(1)} %get-tuple-element.323), channel_id=1, source_target_pairs={{96,80},{80,64},{64,48},{48,32},{32,16},{16,0},{97,81},{81,65},{65... | collective-permute-start | bytes 786440 | tf_op jit(solution)/shard_map/ppermute | solution.py:306
  594.0 10.2 %collective-permute-start.39 = (bf16[16,8192]{1,0:T(8,128)(2,1)S(1)}, bf16[16,8192]{1,0:T(8,128)(2,1)S(1)}, u32[]{:S(2)}, u32[]{:S(2)}) collective-permute-start(bf16[16,8192]{1,0:T(8,128)(2,1)S(1)} %get-tuple-element.330), channel_id=1, source_target_pairs={{80,64},{64,48},{48,32},{32,16},{16,0},{81,65},{65,49},{49,33},{33... | collective-permute-start | bytes 786440 | tf_op jit(solution)/shard_map/ppermute | solution.py:306
  755.1 6.1 backward_step.50
  761.2 6.1 backward_step.51
  769.7 8.2 all-to-all-start.1
  782.9 37.5 %all-to-all-done.1 = bf16[192,16,512]{2,0,1:T(8,128)(2,1)} async-done(((bf16[192,16,512]{2,0,1:T(8,128)(2,1)}), bf16[192,16,512]{2,0,1:T(8,128)(2,1)}, u32[]{:S(2)}, u32[]{:S(2)}) %all-to-all-start.1) | async-done | bytes 3145760 | tf_op jit(solution)/shard_map/all_to_all | solution.py:238
  820.4 9.5 %all-to-all-start = ((bf16[192,16,512]{2,0,1:T(8,128)(2,1)}), bf16[192,16,512]{2,0,1:T(8,128)(2,1)}, u32[]{:S(2)}, u32[]{:S(2)}) async-start(bf16[192,16,512]{2,0,1:T(8,128)(2,1)} %bitcast.55), calls=%async_computation | async-start | bytes 6291456 | tf_op jit(solution)/shard_map/all_to_all | solution.py:238
  830.0 5.4 fusion.1
  835.4 42.8 %all-to-all-done = bf16[192,16,512]{2,0,1:T(8,128)(2,1)} async-done(((bf16[192,16,512]{2,0,1:T(8,128)(2,1)}), bf16[192,16,512]{2,0,1:T(8,128)(2,1)}, u32[]{:S(2)}, u32[]{:S(2)}) %all-to-all-start) | async-done | bytes 3145760 | tf_op jit(solution)/shard_map/all_to_all | solution.py:238
  878.2 5.5 fusion
  (396 shorter events, 525.3 us)
Async XLA Ops:
  7.2 822.8 %all-gather.5.cloned.1.call-start = ((), (), s32[]{:S(2)}) async-start(), calls=%async_computation.3 | async-start | bytes 3342336 | tf_op jit(solution)/shard_map/all_gather | solution.py:234
  73.4 21.7 %collective-permute-start.8 = (bf16[16,8192]{1,0:T(8,128)(2,1)S(1)}, bf16[16,8192]{1,0:T(8,128)(2,1)S(1)}, u32[]{:S(2)}, u32[]{:S(2)}) collective-permute-start(bf16[16,8192]{1,0:T(8,128)(2,1)S(1)} %get-tuple-element.219), channel_id=1, source_target_pairs={{0,16},{16,32},{32,48},{48,64},{64,80},{1,17},{17,33},{33,49},{49,... | collective-permute-start | bytes 786440 | tf_op jit(solution)/shard_map/ppermute | solution.py:271
  79.5 29.1 %collective-permute-start.11 = (bf16[16,8192]{1,0:T(8,128)(2,1)S(1)}, bf16[16,8192]{1,0:T(8,128)(2,1)S(1)}, u32[]{:S(2)}, u32[]{:S(2)}) collective-permute-start(bf16[16,8192]{1,0:T(8,128)(2,1)S(1)} %get-tuple-element.228), channel_id=1, source_target_pairs={{0,16},{16,32},{32,48},{48,64},{64,80},{80,96},{1,17},{17,33},{33,... | collective-permute-start | bytes 786440 | tf_op jit(solution)/shard_map/ppermute | solution.py:271
  98.4 23.0 %collective-permute-start.10 = (bf16[16,8192]{1,0:T(8,128)(2,1)S(1)}, bf16[16,8192]{1,0:T(8,128)(2,1)S(1)}, u32[]{:S(2)}, u32[]{:S(2)}) collective-permute-start(bf16[16,8192]{1,0:T(8,128)(2,1)S(1)} %get-tuple-element.227), channel_id=1, source_target_pairs={{0,16},{16,32},{32,48},{48,64},{64,80},{80,96},{1,17},{17,33},{33,... | collective-permute-start | bytes 786440 | tf_op jit(solution)/shard_map/ppermute | solution.py:271
  111.8 23.0 %collective-permute-start.13 = (bf16[16,8192]{1,0:T(8,128)(2,1)S(1)}, bf16[16,8192]{1,0:T(8,128)(2,1)S(1)}, u32[]{:S(2)}, u32[]{:S(2)}) collective-permute-start(bf16[16,8192]{1,0:T(8,128)(2,1)S(1)} %get-tuple-element.236), channel_id=1, source_target_pairs={{16,32},{32,48},{48,64},{64,80},{80,96},{96,112},{17,33},{33,49},{... | collective-permute-start | bytes 786440 | tf_op jit(solution)/shard_map/ppermute | solution.py:271
  124.6 24.0 %collective-permute-start.12 = (bf16[16,8192]{1,0:T(8,128)(2,1)S(1)}, bf16[16,8192]{1,0:T(8,128)(2,1)S(1)}, u32[]{:S(2)}, u32[]{:S(2)}) collective-permute-start(bf16[16,8192]{1,0:T(8,128)(2,1)S(1)} %get-tuple-element.235), channel_id=1, source_target_pairs={{16,32},{32,48},{48,64},{64,80},{80,96},{96,112},{17,33},{33,49},{... | collective-permute-start | bytes 786440 | tf_op jit(solution)/shard_map/ppermute | solution.py:271
  138.1 24.0 %collective-permute-start.15 = (bf16[16,8192]{1,0:T(8,128)(2,1)S(1)}, bf16[16,8192]{1,0:T(8,128)(2,1)S(1)}, u32[]{:S(2)}, u32[]{:S(2)}) collective-permute-start(bf16[16,8192]{1,0:T(8,128)(2,1)S(1)} %get-tuple-element.244), channel_id=1, source_target_pairs={{32,48},{48,64},{64,80},{80,96},{96,112},{33,49},{49,65},{65,81},{... | collective-permute-start | bytes 786440 | tf_op jit(solution)/shard_map/ppermute | solution.py:271
  151.9 14.1 %collective-permute-start.14 = (bf16[16,8192]{1,0:T(8,128)(2,1)S(1)}, bf16[16,8192]{1,0:T(8,128)(2,1)S(1)}, u32[]{:S(2)}, u32[]{:S(2)}) collective-permute-start(bf16[16,8192]{1,0:T(8,128)(2,1)S(1)} %get-tuple-element.243), channel_id=1, source_target_pairs={{32,48},{48,64},{64,80},{80,96},{96,112},{33,49},{49,65},{65,81},{... | collective-permute-start | bytes 786440 | tf_op jit(solution)/shard_map/ppermute | solution.py:271
  195.8 16.4 %collective-permute-start.22 = (bf16[16,8192]{1,0:T(8,128)(2,1)S(1)}, bf16[16,8192]{1,0:T(8,128)(2,1)S(1)}, u32[]{:S(2)}, u32[]{:S(2)}) collective-permute-start(bf16[16,8192]{1,0:T(8,128)(2,1)S(1)} %get-tuple-element.275), channel_id=1, source_target_pairs={{96,112},{97,113},{98,114},{99,115},{100,116},{101,117},{102,118},... | collective-permute-start | bytes 786440 | tf_op jit(solution)/shard_map/ppermute | solution.py:271
  245.7 24.8 %collective-permute-start.24 = (bf16[16,8192]{1,0:T(8,128)(2,1)S(1)}, bf16[16,8192]{1,0:T(8,128)(2,1)S(1)}, u32[]{:S(2)}, u32[]{:S(2)}) collective-permute-start(bf16[16,8192]{1,0:T(8,128)(2,1)S(1)} %get-tuple-element.287), channel_id=1, source_target_pairs={{112,96},{113,97},{114,98},{115,99},{116,100},{117,101},{118,102},... | collective-permute-start | bytes 786440 | tf_op jit(solution)/shard_map/ppermute | solution.py:306
  269.8 19.5 %collective-permute-start.27 = (bf16[16,8192]{1,0:T(8,128)(2,1)S(1)}, bf16[16,8192]{1,0:T(8,128)(2,1)S(1)}, u32[]{:S(2)}, u32[]{:S(2)}) collective-permute-start(bf16[16,8192]{1,0:T(8,128)(2,1)S(1)} %get-tuple-element.294), channel_id=1, source_target_pairs={{112,96},{96,80},{113,97},{97,81},{114,98},{98,82},{115,99},{99,83... | collective-permute-start | bytes 786440 | tf_op jit(solution)/shard_map/ppermute | solution.py:306
  288.4 21.6 %collective-permute-start.26 = (bf16[16,8192]{1,0:T(8,128)(2,1)S(1)}, bf16[16,8192]{1,0:T(8,128)(2,1)S(1)}, u32[]{:S(2)}, u32[]{:S(2)}) collective-permute-start(bf16[16,8192]{1,0:T(8,128)(2,1)S(1)} %get-tuple-element.293), channel_id=1, source_target_pairs={{112,96},{96,80},{113,97},{97,81},{114,98},{98,82},{115,99},{99,83... | collective-permute-start | bytes 786440 | tf_op jit(solution)/shard_map/ppermute | solution.py:306
  309.3 19.4 %collective-permute-start.29 = (bf16[16,8192]{1,0:T(8,128)(2,1)S(1)}, bf16[16,8192]{1,0:T(8,128)(2,1)S(1)}, u32[]{:S(2)}, u32[]{:S(2)}) collective-permute-start(bf16[16,8192]{1,0:T(8,128)(2,1)S(1)} %get-tuple-element.300), channel_id=1, source_target_pairs={{112,96},{96,80},{80,64},{113,97},{97,81},{81,65},{114,98},{98,82}... | collective-permute-start | bytes 786440 | tf_op jit(solution)/shard_map/ppermute | solution.py:306
  327.9 21.6 %collective-permute-start.28 = (bf16[16,8192]{1,0:T(8,128)(2,1)S(1)}, bf16[16,8192]{1,0:T(8,128)(2,1)S(1)}, u32[]{:S(2)}, u32[]{:S(2)}) collective-permute-start(bf16[16,8192]{1,0:T(8,128)(2,1)S(1)} %get-tuple-element.299), channel_id=1, source_target_pairs={{112,96},{96,80},{80,64},{113,97},{97,81},{81,65},{114,98},{98,82}... | collective-permute-start | bytes 786440 | tf_op jit(solution)/shard_map/ppermute | solution.py:306
  348.9 19.4 %collective-permute-start.31 = (bf16[16,8192]{1,0:T(8,128)(2,1)S(1)}, bf16[16,8192]{1,0:T(8,128)(2,1)S(1)}, u32[]{:S(2)}, u32[]{:S(2)}) collective-permute-start(bf16[16,8192]{1,0:T(8,128)(2,1)S(1)} %get-tuple-element.306), channel_id=1, source_target_pairs={{112,96},{96,80},{80,64},{64,48},{113,97},{97,81},{81,65},{65,49},... | collective-permute-start | bytes 786440 | tf_op jit(solution)/shard_map/ppermute | solution.py:306
  367.5 61.1 %collective-permute-start.30 = (bf16[16,8192]{1,0:T(8,128)(2,1)S(1)}, bf16[16,8192]{1,0:T(8,128)(2,1)S(1)}, u32[]{:S(2)}, u32[]{:S(2)}) collective-permute-start(bf16[16,8192]{1,0:T(8,128)(2,1)S(1)} %get-tuple-element.305), channel_id=1, source_target_pairs={{112,96},{96,80},{80,64},{64,48},{113,97},{97,81},{81,65},{65,49},... | collective-permute-start | bytes 786440 | tf_op jit(solution)/shard_map/ppermute | solution.py:306
  388.3 68.5 %collective-permute-start.33 = (bf16[16,8192]{1,0:T(8,128)(2,1)S(1)}, bf16[16,8192]{1,0:T(8,128)(2,1)S(1)}, u32[]{:S(2)}, u32[]{:S(2)}) collective-permute-start(bf16[16,8192]{1,0:T(8,128)(2,1)S(1)} %get-tuple-element.312), channel_id=1, source_target_pairs={{112,96},{96,80},{80,64},{64,48},{48,32},{113,97},{97,81},{81,65},... | collective-permute-start | bytes 786440 | tf_op jit(solution)/shard_map/ppermute | solution.py:306
  446.4 40.7 %collective-permute-start.32 = (bf16[16,8192]{1,0:T(8,128)(2,1)S(1)}, bf16[16,8192]{1,0:T(8,128)(2,1)S(1)}, u32[]{:S(2)}, u32[]{:S(2)}) collective-permute-start(bf16[16,8192]{1,0:T(8,128)(2,1)S(1)} %get-tuple-element.311), channel_id=1, source_target_pairs={{112,96},{96,80},{80,64},{64,48},{48,32},{113,97},{97,81},{81,65},... | collective-permute-start | bytes 786440 | tf_op jit(solution)/shard_map/ppermute | solution.py:306
  476.9 38.4 %collective-permute-start.35 = (bf16[16,8192]{1,0:T(8,128)(2,1)S(1)}, bf16[16,8192]{1,0:T(8,128)(2,1)S(1)}, u32[]{:S(2)}, u32[]{:S(2)}) collective-permute-start(bf16[16,8192]{1,0:T(8,128)(2,1)S(1)} %get-tuple-element.318), channel_id=1, source_target_pairs={{112,96},{96,80},{80,64},{64,48},{48,32},{32,16},{113,97},{97,81},... | collective-permute-start | bytes 786440 | tf_op jit(solution)/shard_map/ppermute | solution.py:306
  505.0 40.5 %collective-permute-start.34 = (bf16[16,8192]{1,0:T(8,128)(2,1)S(1)}, bf16[16,8192]{1,0:T(8,128)(2,1)S(1)}, u32[]{:S(2)}, u32[]{:S(2)}) collective-permute-start(bf16[16,8192]{1,0:T(8,128)(2,1)S(1)} %get-tuple-element.317), channel_id=1, source_target_pairs={{112,96},{96,80},{80,64},{64,48},{48,32},{32,16},{113,97},{97,81},... | collective-permute-start | bytes 786440 | tf_op jit(solution)/shard_map/ppermute | solution.py:306
  535.3 38.8 %collective-permute-start.37 = (bf16[16,8192]{1,0:T(8,128)(2,1)S(1)}, bf16[16,8192]{1,0:T(8,128)(2,1)S(1)}, u32[]{:S(2)}, u32[]{:S(2)}) collective-permute-start(bf16[16,8192]{1,0:T(8,128)(2,1)S(1)} %get-tuple-element.324), channel_id=1, source_target_pairs={{96,80},{80,64},{64,48},{48,32},{32,16},{16,0},{97,81},{81,65},{65... | collective-permute-start | bytes 786440 | tf_op jit(solution)/shard_map/ppermute | solution.py:306
  563.3 40.9 %collective-permute-start.36 = (bf16[16,8192]{1,0:T(8,128)(2,1)S(1)}, bf16[16,8192]{1,0:T(8,128)(2,1)S(1)}, u32[]{:S(2)}, u32[]{:S(2)}) collective-permute-start(bf16[16,8192]{1,0:T(8,128)(2,1)S(1)} %get-tuple-element.323), channel_id=1, source_target_pairs={{96,80},{80,64},{64,48},{48,32},{32,16},{16,0},{97,81},{81,65},{65... | collective-permute-start | bytes 786440 | tf_op jit(solution)/shard_map/ppermute | solution.py:306
  594.0 19.8 %collective-permute-start.39 = (bf16[16,8192]{1,0:T(8,128)(2,1)S(1)}, bf16[16,8192]{1,0:T(8,128)(2,1)S(1)}, u32[]{:S(2)}, u32[]{:S(2)}) collective-permute-start(bf16[16,8192]{1,0:T(8,128)(2,1)S(1)} %get-tuple-element.330), channel_id=1, source_target_pairs={{80,64},{64,48},{48,32},{32,16},{16,0},{81,65},{65,49},{49,33},{33... | collective-permute-start | bytes 786440 | tf_op jit(solution)/shard_map/ppermute | solution.py:306
  612.4 22.7 %collective-permute-start.38 = (bf16[16,8192]{1,0:T(8,128)(2,1)S(1)}, bf16[16,8192]{1,0:T(8,128)(2,1)S(1)}, u32[]{:S(2)}, u32[]{:S(2)}) collective-permute-start(bf16[16,8192]{1,0:T(8,128)(2,1)S(1)} %get-tuple-element.329), channel_id=1, source_target_pairs={{80,64},{64,48},{48,32},{32,16},{16,0},{81,65},{65,49},{49,33},{33... | collective-permute-start | bytes 786440 | tf_op jit(solution)/shard_map/ppermute | solution.py:306
  643.3 22.9 %collective-permute-start.40 = (bf16[16,8192]{1,0:T(8,128)(2,1)S(1)}, bf16[16,8192]{1,0:T(8,128)(2,1)S(1)}, u32[]{:S(2)}, u32[]{:S(2)}) collective-permute-start(bf16[16,8192]{1,0:T(8,128)(2,1)S(1)} %get-tuple-element.335), channel_id=1, source_target_pairs={{64,48},{48,32},{32,16},{16,0},{65,49},{49,33},{33,17},{17,1},{66,... | collective-permute-start | bytes 786440 | tf_op jit(solution)/shard_map/ppermute | solution.py:306
  674.3 23.6 %collective-permute-start.42 = (bf16[16,8192]{1,0:T(8,128)(2,1)S(1)}, bf16[16,8192]{1,0:T(8,128)(2,1)S(1)}, u32[]{:S(2)}, u32[]{:S(2)}) collective-permute-start(bf16[16,8192]{1,0:T(8,128)(2,1)S(1)} %get-tuple-element.341), channel_id=1, source_target_pairs={{48,32},{32,16},{16,0},{49,33},{33,17},{17,1},{50,34},{34,18},{18,... | collective-permute-start | bytes 786440 | tf_op jit(solution)/shard_map/ppermute | solution.py:306
  696.6 12.2 %collective-permute-start.45 = (bf16[16,8192]{1,0:T(8,128)(2,1)S(1)}, bf16[16,8192]{1,0:T(8,128)(2,1)S(1)}, u32[]{:S(2)}, u32[]{:S(2)}) collective-permute-start(bf16[16,8192]{1,0:T(8,128)(2,1)S(1)} %get-tuple-element.348), channel_id=1, source_target_pairs={{32,16},{16,0},{33,17},{17,1},{34,18},{18,2},{35,19},{19,3},{36,20... | collective-permute-start | bytes 786440 | tf_op jit(solution)/shard_map/ppermute | solution.py:306
  706.1 23.9 %collective-permute-start.44 = (bf16[16,8192]{1,0:T(8,128)(2,1)S(1)}, bf16[16,8192]{1,0:T(8,128)(2,1)S(1)}, u32[]{:S(2)}, u32[]{:S(2)}) collective-permute-start(bf16[16,8192]{1,0:T(8,128)(2,1)S(1)} %get-tuple-element.347), channel_id=1, source_target_pairs={{32,16},{16,0},{33,17},{17,1},{34,18},{18,2},{35,19},{19,3},{36,20... | collective-permute-start | bytes 786440 | tf_op jit(solution)/shard_map/ppermute | solution.py:306
  738.3 22.9 %collective-permute-start.46 = (bf16[16,8192]{1,0:T(8,128)(2,1)S(1)}, bf16[16,8192]{1,0:T(8,128)(2,1)S(1)}, u32[]{:S(2)}, u32[]{:S(2)}) collective-permute-start(bf16[16,8192]{1,0:T(8,128)(2,1)S(1)} %get-tuple-element.353), channel_id=1, source_target_pairs={{16,0},{17,1},{18,2},{19,3},{20,4},{21,5},{22,6},{23,7},{24,8},{25... | collective-permute-start | bytes 786440 | tf_op jit(solution)/shard_map/ppermute | solution.py:306
  769.7 50.7 %all-to-all-start.1 = ((bf16[192,16,512]{2,0,1:T(8,128)(2,1)}), bf16[192,16,512]{2,0,1:T(8,128)(2,1)}, u32[]{:S(2)}, u32[]{:S(2)}) async-start(bf16[192,16,512]{2,0,1:T(8,128)(2,1)} %bitcast.54), calls=%async_computation.1 | async-start | bytes 6291456 | tf_op jit(solution)/shard_map/all_to_all | solution.py:238
  777.8 100.4 %all-gather.3.cloned.1.call-start = ((), (), s32[]{:S(2)}) async-start(), calls=%async_computation.2 | async-start | bytes 3342336 | tf_op jit(solution)/shard_map/all_gather | solution.py:234
  820.4 57.8 %all-to-all-start = ((bf16[192,16,512]{2,0,1:T(8,128)(2,1)}), bf16[192,16,512]{2,0,1:T(8,128)(2,1)}, u32[]{:S(2)}, u32[]{:S(2)}) async-start(bf16[192,16,512]{2,0,1:T(8,128)(2,1)} %bitcast.55), calls=%async_computation | async-start | bytes 6291456 | tf_op jit(solution)/shard_map/all_to_all | solution.py:238
  (137 other events, 939.7 us)
Sparse Core Ops, SparseCore 0:
  219.8 74.0 all-gather.4
  781.7 89.7 all-gather.2

commit v2 on v1

v2 whole, which is shorter than its diff:
```python
import functools

import jax
import jax.numpy as jnp
from jax import lax
from jax.experimental import pallas as pl
from jax.experimental.pallas import tpu as pltpu
from jax.sharding import PartitionSpec as P

EPSILON = 1e-05
SPLIT = 2
SKEW = 2
AUX = 128
TOGETHER = 2

F32 = jnp.float32
BF16 = jnp.bfloat16


def hbm():
    return pl.BlockSpec(memory_space=pltpu.HBM)


def vmem():
    return pl.BlockSpec(memory_space=pltpu.VMEM)


def smem():
    return pl.BlockSpec(memory_space=pltpu.SMEM)


def across(count, body, start):
    def step(j, carry):
        for k in range(TOGETHER):
            carry = body(j * TOGETHER + k, carry)
        return carry

    return lax.fori_loop(0, count // TOGETHER, step, start)


def kept_in(space, *arrays):
    return [pltpu.with_memory_space_constraint(a, space) for a in arrays]


def load_kernel(*refs):
    count = (len(refs) - 1) // 2
    sems = refs[-1]
    copies = [
        pltpu.make_async_copy(refs[k], refs[count + k], sems.at[k]) for k in range(count)
    ]
    for copy in copies:
        copy.start()
    for copy in copies:
        copy.wait()


def resident(*arrays):
    return pl.pallas_call(
        load_kernel,
        out_shape=tuple(pltpu.VMEM(a.shape, a.dtype) for a in arrays),
        in_specs=[hbm()] * len(arrays),
        out_specs=tuple(vmem() for a in arrays),
        scratch_shapes=[pltpu.SemaphoreType.DMA((len(arrays),))],
        compiler_params=pltpu.CompilerParams(vmem_limit_bytes=1 << 20),
        name="resident",
    )(*kept_in(pltpu.HBM, *arrays))


def spread(source, target, sem):
    count, rows, cut = target.shape
    return [
        pltpu.make_async_copy(source.at[:, pl.ds(j * cut, cut)], target.at[j], sem)
        for j in range(count)
    ]


def fetch(fresh, fresh_here, arrived, target, sem):
    moved = pltpu.make_async_copy(arrived, target, sem)
    if fresh is None:
        moved.start()
        moved.wait()
        return

    @pl.when(fresh_here)
    def _():
        copies = spread(fresh, target, sem)
        for copy in copies:
            copy.start()
        moved.wait()

    @pl.when(jnp.logical_not(fresh_here))
    def _():
        moved.start()
        moved.wait()


def block(j, cut):
    return pl.ds(pl.multiple_of(j * cut, cut), cut)


def forward_kernel(tick, chunks, place, plan, arrived, inputs, gain, w_in, w_out, *rest):
    if tick > 0:
        rest = rest[3:]
    send, normed_all, aux_all, hidden_all, x, normed, aux, hidden, sems = rest
    count, rows, cut = x.shape
    width = count * cut
    inner = w_in.shape[1]
    fresh = None
    if tick < chunks:
        slot, part = divmod(tick, SPLIT)
        fresh = inputs.at[plan[slot], pl.ds(part * rows, rows), :]
    fetch(fresh, place[0] == 0, arrived, x, sems.at[0])
    mine = tick - SKEW * place[0]
    active = jnp.logical_and(mine >= 0, mine < chunks)
    at = pl.ds(pl.multiple_of(jnp.clip(mine, 0, chunks - 1) * rows, rows), rows)
    stores = [
        pltpu.make_async_copy(normed, normed_all.at[:, at, :], sems.at[1]),
        pltpu.make_async_copy(aux, aux_all.at[at, :], sems.at[2]),
        pltpu.make_async_copy(hidden, hidden_all.at[at, :], sems.at[3]),
    ]

    def squares(j, total):
        value = x[j].astype(F32)
        return total + value * value

    total = across(count, squares, jnp.zeros((rows, cut), F32))
    inverse = lax.rsqrt(jnp.sum(total, axis=1, keepdims=True) / width + EPSILON)

    def project(j, pre):
        piece = (x[j].astype(F32) * inverse * gain[:, block(j, cut)]).astype(BF16)
        normed[j] = piece
        return pre + jnp.dot(piece, w_in[block(j, cut), :], preferred_element_type=F32)

    pre = across(count, project, jnp.zeros((rows, inner), F32))
    aux[:, :inner] = pre
    aux[:, inner:] = jnp.broadcast_to(inverse, (rows, AUX))
    act = (pre / (1.0 + jnp.exp(-pre))).astype(BF16)
    hidden[...] = act

    @pl.when(active)
    def _():
        for store in stores:
            store.start()

    def expand(j, nothing):
        delta = jnp.dot(act, w_out[:, block(j, cut)], preferred_element_type=F32)
        send[j] = (x[j].astype(F32) + delta).astype(BF16)
        return nothing

    across(count, expand, 0)

    @pl.when(active)
    def _():
        for store in stores:
            store.wait()


def forward_step(tick, chunks, rows, count, place, plan, arrived, inputs, gain, w_in, w_out, kept):
    width, inner = w_in.shape
    cut = width // count
    shapes = (
        jax.ShapeDtypeStruct((count, rows, cut), BF16),
        pltpu.HBM((count, chunks * rows, cut), BF16),
        pltpu.HBM((chunks * rows, inner + AUX), F32),
        pltpu.HBM((chunks * rows, inner), BF16),
    )
    specs = [smem(), smem(), hbm(), hbm(), vmem(), vmem(), vmem()] + [hbm()] * len(kept)
    return pl.pallas_call(
        functools.partial(forward_kernel, tick, chunks),
        out_shape=shapes,
        in_specs=specs,
        out_specs=(vmem(), hbm(), hbm(), hbm()),
        scratch_shapes=[
            pltpu.VMEM((count, rows, cut), BF16),
            pltpu.VMEM((count, rows, cut), BF16),
            pltpu.VMEM((rows, inner + AUX), F32),
            pltpu.VMEM((rows, inner), BF16),
            pltpu.SemaphoreType.DMA((4,)),
        ],
        input_output_aliases={7 + k: 1 + k for k in range(len(kept))},
        compiler_params=pltpu.CompilerParams(vmem_limit_bytes=8 << 20),
        cost_estimate=pl.CostEstimate(
            flops=4 * rows * width * inner, bytes_accessed=10 << 20, transcendentals=0
        ),
        name="forward_step",
    )(
        place,
        plan,
        arrived,
        *kept_in(pltpu.HBM, inputs),
        gain,
        *kept_in(pltpu.VMEM, w_in, w_out),
        *kept_in(pltpu.HBM, *kept),
    )


def backward_kernel(
    tick, chunks, sections, place, arrived, cotangent, normed_all, aux_all, gain, w_in, w_out, *rest
):
    if tick > 0:
        rest = rest[2:]
    send, up_all, grad_all, up, normed, aux, grad, sems = rest
    count, rows, cut = up.shape
    width = count * cut
    inner = w_in.shape[0]
    mine = tick - SKEW * (sections - 1 - place[0])
    active = jnp.logical_and(mine >= 0, mine < chunks)
    at = pl.ds(pl.multiple_of(jnp.clip(mine, 0, chunks - 1) * rows, rows), rows)
    load_normed = pltpu.make_async_copy(normed_all.at[:, at, :], normed, sems.at[1])
    load_normed.start()
    load_aux = pltpu.make_async_copy(aux_all.at[at, :], aux, sems.at[2])
    load_aux.start()
    fresh = None
    if tick < chunks:
        slot, part = divmod(tick, SPLIT)
        fresh = cotangent.at[slot, pl.ds(part * rows, rows), :]
    fetch(fresh, place[0] == sections - 1, arrived, up, sems.at[0])
    store_up = pltpu.make_async_copy(up, up_all.at[:, at, :], sems.at[3])
    store_grad = pltpu.make_async_copy(grad, grad_all.at[at, :], sems.at[4])

    @pl.when(active)
    def _():
        store_up.start()

    def project(j, total):
        return total + jnp.dot(up[j], w_out[block(j, cut), :], preferred_element_type=F32)

    grad_hidden = across(count, project, jnp.zeros((rows, inner), F32))
    load_aux.wait()
    pre = aux[:, :inner]
    inverse = aux[:, inner : inner + 1]
    gate = 1.0 / (1.0 + jnp.exp(-pre))
    grad_pre = (grad_hidden * gate * (1.0 + pre * (1.0 - gate))).astype(BF16)
    grad[...] = grad_pre

    @pl.when(active)
    def _():
        store_grad.start()

    mean = jnp.sum(grad_pre.astype(F32) * pre, axis=1, keepdims=True) / width
    load_normed.wait()

    def expand(j, nothing):
        cols = block(j, cut)
        back = jnp.dot(grad_pre, w_in[:, cols], preferred_element_type=F32)
        scale = gain[:, cols]
        xhat = normed[j].astype(F32) * (1.0 / scale)
        send[j] = (up[j].astype(F32) + inverse * (back * scale - xhat * mean)).astype(BF16)
        return nothing

    across(count, expand, 0)

    @pl.when(active)
    def _():
        store_up.wait()
        store_grad.wait()


def backward_step(
    tick, chunks, rows, sections, place, arrived, cotangent, normed_all, aux_all, gain, w_in, w_out, kept
):
    inner, width = w_in.shape
    count = normed_all.shape[0]
    cut = width // count
    shapes = (
        jax.ShapeDtypeStruct((count, rows, cut), BF16),
        pltpu.HBM((count, chunks * rows, cut), BF16),
        pltpu.HBM((chunks * rows, inner), BF16),
    )
    specs = [smem()] + [hbm()] * 4 + [vmem()] * 3 + [hbm()] * len(kept)
    return pl.pallas_call(
        functools.partial(backward_kernel, tick, chunks, sections),
        out_shape=shapes,
        in_specs=specs,
        out_specs=(vmem(), hbm(), hbm()),
        scratch_shapes=[
            pltpu.VMEM((count, rows, cut), BF16),
            pltpu.VMEM((count, rows, cut), BF16),
            pltpu.VMEM((rows, inner + AUX), F32),
            pltpu.VMEM((rows, inner), BF16),
            pltpu.SemaphoreType.DMA((5,)),
        ],
        input_output_aliases={8 + k: 1 + k for k in range(len(kept))},
        compiler_params=pltpu.CompilerParams(vmem_limit_bytes=8 << 20),
        cost_estimate=pl.CostEstimate(
            flops=4 * rows * width * inner, bytes_accessed=10 << 20, transcendentals=0
        ),
        name="backward_step",
    )(
        place,
        arrived,
        *kept_in(pltpu.HBM, cotangent, normed_all, aux_all),
        gain,
        *kept_in(pltpu.VMEM, w_in, w_out),
        *kept_in(pltpu.HBM, *kept),
    )


def gathered(array, axis):
    return lax.all_gather(array, axis, axis=0, tiled=True)


def columns(array, axis):
    taken = lax.all_to_all(array, axis, split_axis=0, concat_axis=0, tiled=True)
    return taken.reshape(-1, array.shape[-1])


def contracted(left, right):
    return lax.dot_general(left, right, (((0,), (0,)), ((), ())), preferred_element_type=F32)


def per_device(inputs, cotangent, plan_order, norm_gain, weight_in, weight_out):
    sections = lax.axis_size("pipe")
    count = lax.axis_size("dp")
    micro_count, row_count, width = inputs.shape
    rows = row_count // SPLIT
    chunks = micro_count * SPLIT
    ticks = chunks + SKEW * (sections - 1)
    onward = [(s, s + 1) for s in range(sections - 1)]
    back = [(s + 1, s) for s in range(sections - 1)]
    place = lax.axis_index("pipe").astype(jnp.int32).reshape(1)
    plan = plan_order.astype(jnp.int32)
    empty = jnp.zeros((count, rows, width // count), BF16)

    w_in, w_out = resident(weight_in[0], weight_out[0])
    moving = {}
    kept = ()
    for tick in range(ticks):
        arrived = moving.pop(tick, empty)
        send, *kept = forward_step(
            tick, chunks, rows, count, place, plan, arrived, inputs, norm_gain, w_in, w_out, kept
        )
        if tick + SKEW < ticks:
            moving[tick + SKEW] = lax.ppermute(send, "pipe", onward)
    normed_all, aux_all, hidden_all = kept
    normed_cols = columns(normed_all, "dp")
    hidden_rows = gathered(hidden_all, "dp")

    w_in, w_out = resident(weight_in[0].T, weight_out[0].T)
    moving = {}
    kept = ()
    for tick in range(ticks):
        arrived = moving.pop(tick, empty)
        send, *kept = backward_step(
            tick,
            chunks,
            rows,
            sections,
            place,
            arrived,
            cotangent,
            normed_all,
            aux_all,
            norm_gain,
            w_in,
            w_out,
            kept,
        )
        if tick + SKEW < ticks:
            moving[tick + SKEW] = lax.ppermute(send, "pipe", back)
    up_all, grad_all = kept
    up_cols = columns(up_all, "dp")
    grad_rows = gathered(grad_all, "dp")
    total_in = contracted(normed_cols, grad_rows).astype(BF16)
    total_out = contracted(hidden_rows, up_cols).astype(BF16)
    return total_in[None], total_out[None]


def solution(mesh):
    in_specs = (
        P(None, "dp", None),
        P(None, "dp", None),
        P(),
        P("pipe", None),
        P("pipe", None, None),
        P("pipe", None, None),
    )
    out_specs = (P("pipe", "dp", None), P("pipe", None, "dp"))
    return jax.shard_map(
        per_device, mesh=mesh, in_specs=in_specs, out_specs=out_specs, check_vma=False
    )
```

time: 908 us -> 556 us (0.61); the launches traced: 891 us -> 550 us
  local copies, waits for them, and re-layouts: 313 us -> 24 us
  starting transfers between devices: 236 us -> 119 us
  waiting for transfers between devices: 83.7 us -> 120 us
  Pallas kernels: 230 us -> 262 us
    unnamed x234 -> x10, local copies, waits for them, and re-layouts: 305 us -> 24 us
    ppermute x48, starting transfers between devices: 218 us -> 82 us  [the longest x24 50.8 us: per_device(): moving[tick + SKEW] = lax.ppermute(send, 'pipe', onward)]
    ppermute x48, waiting for transfers between devices: 3.33 us -> 33 us  [the longest x24 33 us: per_device(): moving[tick + SKEW] = lax.ppermute(send, 'pipe', back)]
    pallas_call x52, Pallas kernels: 229 us -> 251 us  [the longest x26 138 us: forward_step(): pl.pallas_call(functools.partial(forward_kernel, tick, chunks), out_shape...]
    all_to_all x2, starting transfers between devices: 17.7 us -> 37.4 us  [columns(): taken = lax.all_to_all(array, axis, split_axis=0, concat_axis=0, tiled=True)]
    pallas_call x1 -> x2, Pallas kernels: 1.13 us -> 11.7 us  [resident(): pl.pallas_call(load_kernel, out_shape=tuple((pltpu.VMEM(a.shape, a.dtype)...]
  transfers between devices with their start and end apart: 52 -> 52, of which waited for: 6 -> 25; matrix products, arithmetic and copies ran while one was open for 2% -> 5% of each run, Pallas kernels for 25% -> 45%
where the time goes in v2:
time: 556 us; the launch traced here: 550 us
  Pallas kernels  262 us (47%)
  waiting for transfers between devices  120 us (22%)
  starting transfers between devices  119 us (21%)
  local copies, waits for them, and re-layouts  24 us (4%)
  between operations  15.1 us (3%)
  matrix products  9.95 us (2%)
    pallas_call x26, Pallas kernels, forward_step(): pl.pallas_call(functools.partial(forward_kernel, tick, chunks), out_shape...  138 us
    pallas_call x26, Pallas kernels, backward_step(): pl.pallas_call(functools.partial(backward_kernel, tick, chunks, sections)...  112 us
    all_to_all x2, waiting for transfers between devices, columns(): taken = lax.all_to_all(array, axis, split_axis=0, concat_axis=0, tiled=True)  85.8 us
    ppermute x24, starting transfers between devices, per_device(): moving[tick + SKEW] = lax.ppermute(send, 'pipe', onward)  50.8 us
    all_to_all x2, starting transfers between devices, columns(): taken = lax.all_to_all(array, axis, split_axis=0, concat_axis=0, tiled=True)  37.4 us
    ppermute x24, waiting for transfers between devices, per_device(): moving[tick + SKEW] = lax.ppermute(send, 'pipe', back)  33 us
    ppermute x24, starting transfers between devices, per_device(): moving[tick + SKEW] = lax.ppermute(send, 'pipe', back)  31.2 us
    unnamed x10, local copies, waits for them, and re-layouts  24 us
  transfers between devices with their start and end apart: 52, of which 25 were waited for; matrix products, arithmetic and copies ran while one was open for 5% of the time, Pallas kernels for 45%

profile of v2, /device:TPU:1, one launch (start us, length us, event | category | flops | bytes accessed | tf_op | source)
XLA Modules:
  0.0 550.5 jit_solution(7343574556084443507)
XLA Ops:
  7.2 5.8 %resident.2 = (bf16[8192,512]{1,0:T(8,128)(2,1)S(1)}, bf16[512,8192]{1,0:T(8,128)(2,1)S(1)}) custom-call(bf16[8192,512]{1,0:T(8,128)(2,1)} %bitcast.19, bf16[512,8192]{1,0:T(8,128)(2,1)} %bitcast.20), custom_call_target="tpu_custom_call" | custom-call | tf_op jit(solution)/shard_map/resident/pallas_call | solution.py:58
  13.1 5.7 %forward_step.26 = (bf16[16,16,512]{2,1,0:T(8,128)(2,1)S(1)}, bf16[16,192,512]{2,1,0:T(8,128)(2,1)}, f32[192,640]{1,0:T(8,128)}, bf16[192,512]{1,0:T(8,128)(2,1)}) custom-call(s32[1]{0:T(128)} %bitcast.place, s32[6]{0:T(128)S(1)} %copy-done.3, bf16[16,16,512]{2,1,0:T(8,128)(2,1)S(1)} %broadcast_in_dim.9.arrived, bf16[6,32,8192]{2,1,0:T(8,128)(2,1)} %inputs.51, ...), custom_call_target="tpu_custom_call" | custom-call | flops 268435456 | bytes 10485760 | tf_op jit(solution)/shard_map/forward_step/pallas_call | solution.py:168
  22.1 5.7 %forward_step.27 = (bf16[16,16,512]{2,1,0:T(8,128)(2,1)S(1)}, bf16[16,192,512]{2,1,0:T(8,128)(2,1)}, f32[192,640]{1,0:T(8,128)}, bf16[192,512]{1,0:T(8,128)(2,1)}) custom-call(s32[1]{0:T(128)} %bitcast.place, s32[6]{0:T(128)S(1)} %copy-done.3, ...), custom_call_target="tpu_custom_call", output_to_operand_aliasing={{1}: (7, {}), {2}: (8, {}), {3}: (9, {})} | custom-call | flops 268435456 | bytes 10485760 | tf_op jit(solution)/shard_map/forward_step/pallas_call | solution.py:168
  30.0 5.7 %forward_step.28 = (bf16[16,16,512]{2,1,0:T(8,128)(2,1)S(1)}, bf16[16,192,512]{2,1,0:T(8,128)(2,1)}, f32[192,640]{1,0:T(8,128)}, bf16[192,512]{1,0:T(8,128)(2,1)}) custom-call(s32[1]{0:T(128)} %bitcast.place, s32[6]{0:T(128)S(1)} %copy-done.3, ...), custom_call_target="tpu_custom_call", output_to_operand_aliasing={{1}: (7, {}), {2}: (8, {}), {3}: (9, {})} | custom-call | flops 268435456 | bytes 10485760 | tf_op jit(solution)/shard_map/forward_step/pallas_call | solution.py:168
  38.1 5.7 %forward_step.29 = (bf16[16,16,512]{2,1,0:T(8,128)(2,1)S(1)}, bf16[16,192,512]{2,1,0:T(8,128)(2,1)}, f32[192,640]{1,0:T(8,128)}, bf16[192,512]{1,0:T(8,128)(2,1)}) custom-call(s32[1]{0:T(128)} %bitcast.place, s32[6]{0:T(128)S(1)} %copy-done.3, ...), custom_call_target="tpu_custom_call", output_to_operand_aliasing={{1}: (7, {}), {2}: (8, {}), {3}: (9, {})} | custom-call | flops 268435456 | bytes 10485760 | tf_op jit(solution)/shard_map/forward_step/pallas_call | solution.py:168
  46.0 5.7 %forward_step.30 = (bf16[16,16,512]{2,1,0:T(8,128)(2,1)S(1)}, bf16[16,192,512]{2,1,0:T(8,128)(2,1)}, f32[192,640]{1,0:T(8,128)}, bf16[192,512]{1,0:T(8,128)(2,1)}) custom-call(s32[1]{0:T(128)} %bitcast.place, s32[6]{0:T(128)S(1)} %copy-done.3, ...), custom_call_target="tpu_custom_call", output_to_operand_aliasing={{1}: (7, {}), {2}: (8, {}), {3}: (9, {})} | custom-call | flops 268435456 | bytes 10485760 | tf_op jit(solution)/shard_map/forward_step/pallas_call | solution.py:168
  54.1 5.7 %forward_step.31 = (bf16[16,16,512]{2,1,0:T(8,128)(2,1)S(1)}, bf16[16,192,512]{2,1,0:T(8,128)(2,1)}, f32[192,640]{1,0:T(8,128)}, bf16[192,512]{1,0:T(8,128)(2,1)}) custom-call(s32[1]{0:T(128)} %bitcast.place, s32[6]{0:T(128)S(1)} %copy-done.3, ...), custom_call_target="tpu_custom_call", output_to_operand_aliasing={{1}: (7, {}), {2}: (8, {}), {3}: (9, {})} | custom-call | flops 268435456 | bytes 10485760 | tf_op jit(solution)/shard_map/forward_step/pallas_call | solution.py:168
  61.8 5.7 %forward_step.32 = (bf16[16,16,512]{2,1,0:T(8,128)(2,1)S(1)}, bf16[16,192,512]{2,1,0:T(8,128)(2,1)}, f32[192,640]{1,0:T(8,128)}, bf16[192,512]{1,0:T(8,128)(2,1)}) custom-call(s32[1]{0:T(128)} %bitcast.place, s32[6]{0:T(128)S(1)} %copy-done.3, ...), custom_call_target="tpu_custom_call", output_to_operand_aliasing={{1}: (7, {}), {2}: (8, {}), {3}: (9, {})} | custom-call | flops 268435456 | bytes 10485760 | tf_op jit(solution)/shard_map/forward_step/pallas_call | solution.py:168
  69.9 5.7 %forward_step.33 = (bf16[16,16,512]{2,1,0:T(8,128)(2,1)S(1)}, bf16[16,192,512]{2,1,0:T(8,128)(2,1)}, f32[192,640]{1,0:T(8,128)}, bf16[192,512]{1,0:T(8,128)(2,1)}) custom-call(s32[1]{0:T(128)} %bitcast.place, s32[6]{0:T(128)S(1)} %copy-done.3, ...), custom_call_target="tpu_custom_call", output_to_operand_aliasing={{1}: (7, {}), {2}: (8, {}), {3}: (9, {})} | custom-call | flops 268435456 | bytes 10485760 | tf_op jit(solution)/shard_map/forward_step/pallas_call | solution.py:168
  76.9 5.7 %forward_step.34 = (bf16[16,16,512]{2,1,0:T(8,128)(2,1)S(1)}, bf16[16,192,512]{2,1,0:T(8,128)(2,1)}, f32[192,640]{1,0:T(8,128)}, bf16[192,512]{1,0:T(8,128)(2,1)}) custom-call(s32[1]{0:T(128)} %bitcast.place, s32[6]{0:T(128)S(1)} %copy-done.3, ...), custom_call_target="tpu_custom_call", output_to_operand_aliasing={{1}: (7, {}), {2}: (8, {}), {3}: (9, {})} | custom-call | flops 268435456 | bytes 10485760 | tf_op jit(solution)/shard_map/forward_step/pallas_call | solution.py:168
  84.4 5.7 %forward_step.35 = (bf16[16,16,512]{2,1,0:T(8,128)(2,1)S(1)}, bf16[16,192,512]{2,1,0:T(8,128)(2,1)}, f32[192,640]{1,0:T(8,128)}, bf16[192,512]{1,0:T(8,128)(2,1)}) custom-call(s32[1]{0:T(128)} %bitcast.place, s32[6]{0:T(128)S(1)} %copy-done.3, ...), custom_call_target="tpu_custom_call", output_to_operand_aliasing={{1}: (7, {}), {2}: (8, {}), {3}: (9, {})} | custom-call | flops 268435456 | bytes 10485760 | tf_op jit(solution)/shard_map/forward_step/pallas_call | solution.py:168
  91.5 5.7 %forward_step.36 = (bf16[16,16,512]{2,1,0:T(8,128)(2,1)S(1)}, bf16[16,192,512]{2,1,0:T(8,128)(2,1)}, f32[192,640]{1,0:T(8,128)}, bf16[192,512]{1,0:T(8,128)(2,1)}) custom-call(s32[1]{0:T(128)} %bitcast.place, s32[6]{0:T(128)S(1)} %copy-done.3, ...), custom_call_target="tpu_custom_call", output_to_operand_aliasing={{1}: (7, {}), {2}: (8, {}), {3}: (9, {})} | custom-call | flops 268435456 | bytes 10485760 | tf_op jit(solution)/shard_map/forward_step/pallas_call | solution.py:168
  98.6 5.7 %forward_step.37 = (bf16[16,16,512]{2,1,0:T(8,128)(2,1)S(1)}, bf16[16,192,512]{2,1,0:T(8,128)(2,1)}, f32[192,640]{1,0:T(8,128)}, bf16[192,512]{1,0:T(8,128)(2,1)}) custom-call(s32[1]{0:T(128)} %bitcast.place, s32[6]{0:T(128)S(1)} %copy-done.3, ...), custom_call_target="tpu_custom_call", output_to_operand_aliasing={{1}: (7, {}), {2}: (8, {}), {3}: (9, {})} | custom-call | flops 268435456 | bytes 10485760 | tf_op jit(solution)/shard_map/forward_step/pallas_call | solution.py:168
  105.6 4.9 forward_step.38
  111.8 4.9 forward_step.39
  118.6 4.9 forward_step.40
  125.4 4.9 forward_step.41
  132.3 4.9 forward_step.42
  139.1 4.9 forward_step.43
  191.6 5.6 %forward_step.50 = (bf16[16,16,512]{2,1,0:T(8,128)(2,1)}, bf16[16,192,512]{2,1,0:T(8,128)(2,1)}, f32[192,640]{1,0:T(8,128)}, bf16[192,512]{1,0:T(8,128)(2,1)}) custom-call(s32[1]{0:T(128)} %bitcast.place, s32[6]{0:T(128)S(1)} %copy-done.3, ...), custom_call_target="tpu_custom_call", output_to_operand_aliasing={{1}: (7, {}), {2}: (8, {}), {3}: (9, {})} | custom-call | flops 268435456 | bytes 10485760 | tf_op jit(solution)/shard_map/forward_step/pallas_call | solution.py:168
  197.2 5.6 %forward_step.51 = (bf16[16,16,512]{2,1,0:T(8,128)(2,1)}, bf16[16,192,512]{2,1,0:T(8,128)(2,1)}, f32[192,640]{1,0:T(8,128)}, bf16[192,512]{1,0:T(8,128)(2,1)}) custom-call(s32[1]{0:T(128)} %bitcast.place, s32[6]{0:T(128)S(1)} %copy-done.3, ...), custom_call_target="tpu_custom_call", output_to_operand_aliasing={{1}: (7, {}), {2}: (8, {}), {3}: (9, {})} | custom-call | flops 268435456 | bytes 10485760 | tf_op jit(solution)/shard_map/forward_step/pallas_call | solution.py:168
  202.8 12.0 %copy.133 = bf16[1,8192,512]{1,2,0:T(8,128)(2,1)} copy(bf16[1,8192,512]{2,1,0:T(8,128)(2,1)} %param.10) | data formatting | bytes 16777216 | tf_op args[4]
  214.8 12.0 %copy.134 = bf16[1,512,8192]{1,2,0:T(8,128)(2,1)} copy(bf16[1,512,8192]{2,1,0:T(8,128)(2,1)} %param.11) | data formatting | bytes 16777216 | tf_op args[5]
  226.8 5.9 %resident.3 = (bf16[512,8192]{1,0:T(8,128)(2,1)S(1)}, bf16[8192,512]{1,0:T(8,128)(2,1)S(1)}) custom-call(bf16[512,8192]{1,0:T(8,128)(2,1)} %bitcast.21, bf16[8192,512]{1,0:T(8,128)(2,1)} %bitcast.22), custom_call_target="tpu_custom_call" | custom-call | tf_op jit(solution)/shard_map/resident/pallas_call | solution.py:58
  249.6 8.1 %collective-permute-done.24.arrived = bf16[16,16,512]{2,1,0:T(8,128)(2,1)S(1)} collective-permute-done((bf16[16,16,512]{2,1,0:T(8,128)(2,1)S(1)}, bf16[16,16,512]{2,1,0:T(8,128)(2,1)S(1)}, u32[]{:S(2)}, u32[]{:S(2)}) %collective-permute-start.24) | collective-permute-done | bytes 262176 | tf_op jit(solution)/shard_map/ppermute | solution.py:360
  398.5 5.0 backward_step.50
  404.7 5.0 backward_step.51
  409.7 26.9 %all-to-all-start.1 = ((bf16[16,192,512]{2,1,0:T(8,128)(2,1)}), bf16[16,192,512]{2,1,0:T(8,128)(2,1)S(1)}, u32[]{:S(2)}, u32[]{:S(2)}) async-start(bf16[16,192,512]{2,1,0:T(8,128)(2,1)} %get-tuple-element.365), calls=%async_computation.1 | async-start | bytes 6291456 | tf_op jit(solution)/shard_map/all_to_all | solution.py:304
  437.3 42.1 %all-to-all-done.1 = bf16[16,192,512]{2,1,0:T(8,128)(2,1)S(1)} async-done(((bf16[16,192,512]{2,1,0:T(8,128)(2,1)}), bf16[16,192,512]{2,1,0:T(8,128)(2,1)S(1)}, u32[]{:S(2)}, u32[]{:S(2)}) %all-to-all-start.1) | async-done | bytes 3145760 | tf_op jit(solution)/shard_map/all_to_all | solution.py:304
  479.4 10.5 %all-to-all-start = ((bf16[16,192,512]{2,1,0:T(8,128)(2,1)}), bf16[16,192,512]{2,1,0:T(8,128)(2,1)}, u32[]{:S(2)}, u32[]{:S(2)}) async-start(bf16[16,192,512]{2,1,0:T(8,128)(2,1)} %get-tuple-element.285.normed_all), calls=%async_computation | async-start | bytes 6291456 | tf_op jit(solution)/shard_map/all_to_all | solution.py:304
  494.4 43.8 %all-to-all-done = bf16[16,192,512]{2,1,0:T(8,128)(2,1)} async-done(((bf16[16,192,512]{2,1,0:T(8,128)(2,1)}), bf16[16,192,512]{2,1,0:T(8,128)(2,1)}, u32[]{:S(2)}, u32[]{:S(2)}) %all-to-all-start) | async-done | bytes 3145760 | tf_op jit(solution)/shard_map/all_to_all | solution.py:304
  538.2 5.5 fusion
  (141 shorter events, 244.0 us)
Async XLA Ops:
  7.2 482.8 %all-gather.5.cloned.1.call-start = ((), (), s32[]{:S(2)}) async-start(), calls=%async_computation.3 | async-start | bytes 3342336 | tf_op jit(solution)/shard_map/all_gather | solution.py:300
  18.8 11.1 %collective-permute-start.1 = (bf16[16,16,512]{2,1,0:T(8,128)(2,1)S(1)}, bf16[16,16,512]{2,1,0:T(8,128)(2,1)S(1)}, u32[]{:S(2)}, u32[]{:S(2)}) collective-permute-start(bf16[16,16,512]{2,1,0:T(8,128)(2,1)S(1)} %get-tuple-element.190), channel_id=1, source_target_pairs={{0,16},{16,32},{32,48},{48,64},{64,80},{80,96},{96,112},{1,17},{17... | collective-permute-start | bytes 786440 | tf_op jit(solution)/shard_map/ppermute | solution.py:334
  27.8 10.3 %collective-permute-start = (bf16[16,16,512]{2,1,0:T(8,128)(2,1)S(1)}, bf16[16,16,512]{2,1,0:T(8,128)(2,1)S(1)}, u32[]{:S(2)}, u32[]{:S(2)}) collective-permute-start(bf16[16,16,512]{2,1,0:T(8,128)(2,1)S(1)} %get-tuple-element.189), channel_id=1, source_target_pairs={{0,16},{16,32},{32,48},{48,64},{64,80},{80,96},{96,112},{1,17},{17... | collective-permute-start | bytes 786440 | tf_op jit(solution)/shard_map/ppermute | solution.py:334
  35.7 10.3 %collective-permute-start.3 = (bf16[16,16,512]{2,1,0:T(8,128)(2,1)S(1)}, bf16[16,16,512]{2,1,0:T(8,128)(2,1)S(1)}, u32[]{:S(2)}, u32[]{:S(2)}) collective-permute-start(bf16[16,16,512]{2,1,0:T(8,128)(2,1)S(1)} %get-tuple-element.198), channel_id=1, source_target_pairs={{0,16},{16,32},{32,48},{48,64},{64,80},{80,96},{96,112},{1,17},{17... | collective-permute-start | bytes 786440 | tf_op jit(solution)/shard_map/ppermute | solution.py:334
  43.8 10.3 %collective-permute-start.2 = (bf16[16,16,512]{2,1,0:T(8,128)(2,1)S(1)}, bf16[16,16,512]{2,1,0:T(8,128)(2,1)S(1)}, u32[]{:S(2)}, u32[]{:S(2)}) collective-permute-start(bf16[16,16,512]{2,1,0:T(8,128)(2,1)S(1)} %get-tuple-element.197), channel_id=1, source_target_pairs={{0,16},{16,32},{32,48},{48,64},{64,80},{80,96},{96,112},{1,17},{17... | collective-permute-start | bytes 786440 | tf_op jit(solution)/shard_map/ppermute | solution.py:334
  51.8 10.0 %collective-permute-start.5 = (bf16[16,16,512]{2,1,0:T(8,128)(2,1)S(1)}, bf16[16,16,512]{2,1,0:T(8,128)(2,1)S(1)}, u32[]{:S(2)}, u32[]{:S(2)}) collective-permute-start(bf16[16,16,512]{2,1,0:T(8,128)(2,1)S(1)} %get-tuple-element.206), channel_id=1, source_target_pairs={{0,16},{16,32},{32,48},{48,64},{64,80},{80,96},{96,112},{1,17},{17... | collective-permute-start | bytes 786440 | tf_op jit(solution)/shard_map/ppermute | solution.py:334
  59.9 10.0 %collective-permute-start.4 = (bf16[16,16,512]{2,1,0:T(8,128)(2,1)S(1)}, bf16[16,16,512]{2,1,0:T(8,128)(2,1)S(1)}, u32[]{:S(2)}, u32[]{:S(2)}) collective-permute-start(bf16[16,16,512]{2,1,0:T(8,128)(2,1)S(1)} %get-tuple-element.205), channel_id=1, source_target_pairs={{0,16},{16,32},{32,48},{48,64},{64,80},{80,96},{96,112},{1,17},{17... | collective-permute-start | bytes 786440 | tf_op jit(solution)/shard_map/ppermute | solution.py:334
  67.5 9.4 %collective-permute-start.7 = (bf16[16,16,512]{2,1,0:T(8,128)(2,1)S(1)}, bf16[16,16,512]{2,1,0:T(8,128)(2,1)S(1)}, u32[]{:S(2)}, u32[]{:S(2)}) collective-permute-start(bf16[16,16,512]{2,1,0:T(8,128)(2,1)S(1)} %get-tuple-element.214), channel_id=1, source_target_pairs={{0,16},{16,32},{32,48},{48,64},{64,80},{80,96},{96,112},{1,17},{17... | collective-permute-start | bytes 786440 | tf_op jit(solution)/shard_map/ppermute | solution.py:334
  137.2 10.0 %collective-permute-start.17 = (bf16[16,16,512]{2,1,0:T(8,128)(2,1)S(1)}, bf16[16,16,512]{2,1,0:T(8,128)(2,1)S(1)}, u32[]{:S(2)}, u32[]{:S(2)}) collective-permute-start(bf16[16,16,512]{2,1,0:T(8,128)(2,1)S(1)} %get-tuple-element.254), channel_id=1, source_target_pairs={{0,16},{16,32},{32,48},{48,64},{64,80},{80,96},{96,112},{1,17},{17... | collective-permute-start | bytes 786440 | tf_op jit(solution)/shard_map/ppermute | solution.py:334
  144.0 10.0 %collective-permute-start.16 = (bf16[16,16,512]{2,1,0:T(8,128)(2,1)S(1)}, bf16[16,16,512]{2,1,0:T(8,128)(2,1)S(1)}, u32[]{:S(2)}, u32[]{:S(2)}) collective-permute-start(bf16[16,16,512]{2,1,0:T(8,128)(2,1)S(1)} %get-tuple-element.253), channel_id=1, source_target_pairs={{0,16},{16,32},{32,48},{48,64},{64,80},{80,96},{96,112},{1,17},{17... | collective-permute-start | bytes 786440 | tf_op jit(solution)/shard_map/ppermute | solution.py:334
  152.0 10.8 %collective-permute-start.19 = (bf16[16,16,512]{2,1,0:T(8,128)(2,1)S(1)}, bf16[16,16,512]{2,1,0:T(8,128)(2,1)S(1)}, u32[]{:S(2)}, u32[]{:S(2)}) collective-permute-start(bf16[16,16,512]{2,1,0:T(8,128)(2,1)S(1)} %get-tuple-element.262), channel_id=1, source_target_pairs={{0,16},{16,32},{32,48},{48,64},{64,80},{80,96},{96,112},{1,17},{17... | collective-permute-start | bytes 786440 | tf_op jit(solution)/shard_map/ppermute | solution.py:334
  158.9 10.8 %collective-permute-start.18 = (bf16[16,16,512]{2,1,0:T(8,128)(2,1)S(1)}, bf16[16,16,512]{2,1,0:T(8,128)(2,1)S(1)}, u32[]{:S(2)}, u32[]{:S(2)}) collective-permute-start(bf16[16,16,512]{2,1,0:T(8,128)(2,1)S(1)} %get-tuple-element.261), channel_id=1, source_target_pairs={{0,16},{16,32},{32,48},{48,64},{64,80},{80,96},{96,112},{1,17},{17... | collective-permute-start | bytes 786440 | tf_op jit(solution)/shard_map/ppermute | solution.py:334
  167.7 9.9 %collective-permute-start.21 = (bf16[16,16,512]{2,1,0:T(8,128)(2,1)S(1)}, bf16[16,16,512]{2,1,0:T(8,128)(2,1)S(1)}, u32[]{:S(2)}, u32[]{:S(2)}) collective-permute-start(bf16[16,16,512]{2,1,0:T(8,128)(2,1)S(1)} %get-tuple-element.270), channel_id=1, source_target_pairs={{0,16},{16,32},{32,48},{48,64},{64,80},{80,96},{96,112},{1,17},{17... | collective-permute-start | bytes 786440 | tf_op jit(solution)/shard_map/ppermute | solution.py:334
  174.5 9.9 %collective-permute-start.20 = (bf16[16,16,512]{2,1,0:T(8,128)(2,1)S(1)}, bf16[16,16,512]{2,1,0:T(8,128)(2,1)S(1)}, u32[]{:S(2)}, u32[]{:S(2)}) collective-permute-start(bf16[16,16,512]{2,1,0:T(8,128)(2,1)S(1)} %get-tuple-element.269), channel_id=1, source_target_pairs={{0,16},{16,32},{32,48},{48,64},{64,80},{80,96},{96,112},{1,17},{17... | collective-permute-start | bytes 786440 | tf_op jit(solution)/shard_map/ppermute | solution.py:334
  182.5 9.2 %collective-permute-start.23 = (bf16[16,16,512]{2,1,0:T(8,128)(2,1)S(1)}, bf16[16,16,512]{2,1,0:T(8,128)(2,1)S(1)}, u32[]{:S(2)}, u32[]{:S(2)}) collective-permute-start(bf16[16,16,512]{2,1,0:T(8,128)(2,1)S(1)} %get-tuple-element.278), channel_id=1, source_target_pairs={{0,16},{16,32},{32,48},{48,64},{64,80},{80,96},{96,112},{1,17},{17... | collective-permute-start | bytes 786440 | tf_op jit(solution)/shard_map/ppermute | solution.py:334
  242.6 15.1 %collective-permute-start.24 = (bf16[16,16,512]{2,1,0:T(8,128)(2,1)S(1)}, bf16[16,16,512]{2,1,0:T(8,128)(2,1)S(1)}, u32[]{:S(2)}, u32[]{:S(2)}) collective-permute-start(bf16[16,16,512]{2,1,0:T(8,128)(2,1)S(1)} %get-tuple-element.291), channel_id=1, source_target_pairs={{16,0},{32,16},{48,32},{64,48},{80,64},{96,80},{112,96},{17,1},{33... | collective-permute-start | bytes 786440 | tf_op jit(solution)/shard_map/ppermute | solution.py:360
  248.3 15.2 %collective-permute-start.27 = (bf16[16,16,512]{2,1,0:T(8,128)(2,1)S(1)}, bf16[16,16,512]{2,1,0:T(8,128)(2,1)S(1)}, u32[]{:S(2)}, u32[]{:S(2)}) collective-permute-start(bf16[16,16,512]{2,1,0:T(8,128)(2,1)S(1)} %get-tuple-element.298), channel_id=1, source_target_pairs={{16,0},{32,16},{48,32},{64,48},{80,64},{96,80},{112,96},{17,1},{33... | collective-permute-start | bytes 786440 | tf_op jit(solution)/shard_map/ppermute | solution.py:360
  286.1 9.6 %collective-permute-start.30 = (bf16[16,16,512]{2,1,0:T(8,128)(2,1)S(1)}, bf16[16,16,512]{2,1,0:T(8,128)(2,1)S(1)}, u32[]{:S(2)}, u32[]{:S(2)}) collective-permute-start(bf16[16,16,512]{2,1,0:T(8,128)(2,1)S(1)} %get-tuple-element.309), channel_id=1, source_target_pairs={{16,0},{32,16},{48,32},{64,48},{80,64},{96,80},{112,96},{17,1},{33... | collective-permute-start | bytes 786440 | tf_op jit(solution)/shard_map/ppermute | solution.py:360
  292.6 9.4 %collective-permute-start.33 = (bf16[16,16,512]{2,1,0:T(8,128)(2,1)S(1)}, bf16[16,16,512]{2,1,0:T(8,128)(2,1)S(1)}, u32[]{:S(2)}, u32[]{:S(2)}) collective-permute-start(bf16[16,16,512]{2,1,0:T(8,128)(2,1)S(1)} %get-tuple-element.316), channel_id=1, source_target_pairs={{16,0},{32,16},{48,32},{64,48},{80,64},{96,80},{112,96},{17,1},{33... | collective-permute-start | bytes 786440 | tf_op jit(solution)/shard_map/ppermute | solution.py:360
  300.0 10.7 %collective-permute-start.32 = (bf16[16,16,512]{2,1,0:T(8,128)(2,1)S(1)}, bf16[16,16,512]{2,1,0:T(8,128)(2,1)S(1)}, u32[]{:S(2)}, u32[]{:S(2)}) collective-permute-start(bf16[16,16,512]{2,1,0:T(8,128)(2,1)S(1)} %get-tuple-element.315), channel_id=1, source_target_pairs={{16,0},{32,16},{48,32},{64,48},{80,64},{96,80},{112,96},{17,1},{33... | collective-permute-start | bytes 786440 | tf_op jit(solution)/shard_map/ppermute | solution.py:360
  306.2 10.7 %collective-permute-start.35 = (bf16[16,16,512]{2,1,0:T(8,128)(2,1)S(1)}, bf16[16,16,512]{2,1,0:T(8,128)(2,1)S(1)}, u32[]{:S(2)}, u32[]{:S(2)}) collective-permute-start(bf16[16,16,512]{2,1,0:T(8,128)(2,1)S(1)} %get-tuple-element.322), channel_id=1, source_target_pairs={{16,0},{32,16},{48,32},{64,48},{80,64},{96,80},{112,96},{17,1},{33... | collective-permute-start | bytes 786440 | tf_op jit(solution)/shard_map/ppermute | solution.py:360
  315.0 11.1 %collective-permute-start.34 = (bf16[16,16,512]{2,1,0:T(8,128)(2,1)S(1)}, bf16[16,16,512]{2,1,0:T(8,128)(2,1)S(1)}, u32[]{:S(2)}, u32[]{:S(2)}) collective-permute-start(bf16[16,16,512]{2,1,0:T(8,128)(2,1)S(1)} %get-tuple-element.321), channel_id=1, source_target_pairs={{16,0},{32,16},{48,32},{64,48},{80,64},{96,80},{112,96},{17,1},{33... | collective-permute-start | bytes 786440 | tf_op jit(solution)/shard_map/ppermute | solution.py:360
  321.2 11.1 %collective-permute-start.37 = (bf16[16,16,512]{2,1,0:T(8,128)(2,1)S(1)}, bf16[16,16,512]{2,1,0:T(8,128)(2,1)S(1)}, u32[]{:S(2)}, u32[]{:S(2)}) collective-permute-start(bf16[16,16,512]{2,1,0:T(8,128)(2,1)S(1)} %get-tuple-element.328), channel_id=1, source_target_pairs={{16,0},{32,16},{48,32},{64,48},{80,64},{96,80},{112,96},{17,1},{33... | collective-permute-start | bytes 786440 | tf_op jit(solution)/shard_map/ppermute | solution.py:360
  330.3 9.3 %collective-permute-start.36 = (bf16[16,16,512]{2,1,0:T(8,128)(2,1)S(1)}, bf16[16,16,512]{2,1,0:T(8,128)(2,1)S(1)}, u32[]{:S(2)}, u32[]{:S(2)}) collective-permute-start(bf16[16,16,512]{2,1,0:T(8,128)(2,1)S(1)} %get-tuple-element.327), channel_id=1, source_target_pairs={{16,0},{32,16},{48,32},{64,48},{80,64},{96,80},{112,96},{17,1},{33... | collective-permute-start | bytes 786440 | tf_op jit(solution)/shard_map/ppermute | solution.py:360
  336.6 9.3 %collective-permute-start.39 = (bf16[16,16,512]{2,1,0:T(8,128)(2,1)S(1)}, bf16[16,16,512]{2,1,0:T(8,128)(2,1)S(1)}, u32[]{:S(2)}, u32[]{:S(2)}) collective-permute-start(bf16[16,16,512]{2,1,0:T(8,128)(2,1)S(1)} %get-tuple-element.334), channel_id=1, source_target_pairs={{16,0},{32,16},{48,32},{64,48},{80,64},{96,80},{112,96},{17,1},{33... | collective-permute-start | bytes 786440 | tf_op jit(solution)/shard_map/ppermute | solution.py:360
  374.9 9.0 %collective-permute-start.45 = (bf16[16,16,512]{2,1,0:T(8,128)(2,1)S(1)}, bf16[16,16,512]{2,1,0:T(8,128)(2,1)S(1)}, u32[]{:S(2)}, u32[]{:S(2)}) collective-permute-start(bf16[16,16,512]{2,1,0:T(8,128)(2,1)S(1)} %get-tuple-element.352), channel_id=1, source_target_pairs={{16,0},{32,16},{48,32},{64,48},{80,64},{96,80},{112,96},{17,1},{33... | collective-permute-start | bytes 786440 | tf_op jit(solution)/shard_map/ppermute | solution.py:360
  381.1 9.1 %collective-permute-start.44 = (bf16[16,16,512]{2,1,0:T(8,128)(2,1)S(1)}, bf16[16,16,512]{2,1,0:T(8,128)(2,1)S(1)}, u32[]{:S(2)}, u32[]{:S(2)}) collective-permute-start(bf16[16,16,512]{2,1,0:T(8,128)(2,1)S(1)} %get-tuple-element.351), channel_id=1, source_target_pairs={{16,0},{32,16},{48,32},{64,48},{80,64},{96,80},{112,96},{17,1},{33... | collective-permute-start | bytes 786440 | tf_op jit(solution)/shard_map/ppermute | solution.py:360
  388.2 10.2 %collective-permute-start.47 = (bf16[16,16,512]{2,1,0:T(8,128)(2,1)S(1)}, bf16[16,16,512]{2,1,0:T(8,128)(2,1)S(1)}, u32[]{:S(2)}, u32[]{:S(2)}) collective-permute-start(bf16[16,16,512]{2,1,0:T(8,128)(2,1)S(1)} %get-tuple-element.358), channel_id=1, source_target_pairs={{16,0},{32,16},{48,32},{64,48},{80,64},{96,80},{112,96},{17,1},{33... | collective-permute-start | bytes 786440 | tf_op jit(solution)/shard_map/ppermute | solution.py:360
  394.5 10.3 %collective-permute-start.46 = (bf16[16,16,512]{2,1,0:T(8,128)(2,1)S(1)}, bf16[16,16,512]{2,1,0:T(8,128)(2,1)S(1)}, u32[]{:S(2)}, u32[]{:S(2)}) collective-permute-start(bf16[16,16,512]{2,1,0:T(8,128)(2,1)S(1)} %get-tuple-element.357), channel_id=1, source_target_pairs={{16,0},{32,16},{48,32},{64,48},{80,64},{96,80},{112,96},{17,1},{33... | collective-permute-start | bytes 786440 | tf_op jit(solution)/shard_map/ppermute | solution.py:360
  409.7 69.7 %all-to-all-start.1 = ((bf16[16,192,512]{2,1,0:T(8,128)(2,1)}), bf16[16,192,512]{2,1,0:T(8,128)(2,1)S(1)}, u32[]{:S(2)}, u32[]{:S(2)}) async-start(bf16[16,192,512]{2,1,0:T(8,128)(2,1)} %get-tuple-element.365), calls=%async_computation.1 | async-start | bytes 6291456 | tf_op jit(solution)/shard_map/all_to_all | solution.py:304
  436.6 101.6 %all-gather.3.cloned.1.call-start = ((), (), s32[]{:S(2)}) async-start(), calls=%async_computation.2 | async-start | bytes 3342336 | tf_op jit(solution)/shard_map/all_gather | solution.py:300
  479.4 58.8 %all-to-all-start = ((bf16[16,192,512]{2,1,0:T(8,128)(2,1)}), bf16[16,192,512]{2,1,0:T(8,128)(2,1)}, u32[]{:S(2)}, u32[]{:S(2)}) async-start(bf16[16,192,512]{2,1,0:T(8,128)(2,1)} %get-tuple-element.285.normed_all), calls=%async_computation | async-start | bytes 6291456 | tf_op jit(solution)/shard_map/all_to_all | solution.py:304
  (24 other events, 190.2 us)
Sparse Core Ops, SparseCore 0:
  202.9 72.6 all-gather.4
  439.9 91.6 all-gather.2

commit v3 on v2

v3 whole, which is shorter than its diff:
```python
import functools

import jax
import jax.numpy as jnp
from jax import lax
from jax.experimental import pallas as pl
from jax.experimental.pallas import tpu as pltpu
from jax.sharding import PartitionSpec as P

EPSILON = 1e-05
CHUNKS = 8
SKEW = 2
AUX = 128
TOGETHER = 4

PARTS = 2
TIED = 12

F32 = jnp.float32
BF16 = jnp.bfloat16


def hbm():
    return pl.BlockSpec(memory_space=pltpu.HBM)


def vmem():
    return pl.BlockSpec(memory_space=pltpu.VMEM)


def smem():
    return pl.BlockSpec(memory_space=pltpu.SMEM)


def across(count, body, start):
    def step(j, carry):
        for k in range(TOGETHER):
            carry = body(j * TOGETHER + k, carry)
        return carry

    return lax.fori_loop(0, count // TOGETHER, step, start)


def kept_in(space, *arrays):
    return [pltpu.with_memory_space_constraint(a, space) for a in arrays]


def load_kernel(*refs):
    count = (len(refs) - 1) // 2
    sems = refs[-1]
    copies = [
        pltpu.make_async_copy(refs[k], refs[count + k], sems.at[k]) for k in range(count)
    ]
    for copy in copies:
        copy.start()
    for copy in copies:
        copy.wait()


def resident(*arrays):
    return pl.pallas_call(
        load_kernel,
        out_shape=tuple(pltpu.VMEM(a.shape, a.dtype) for a in arrays),
        in_specs=[hbm()] * len(arrays),
        out_specs=tuple(vmem() for a in arrays),
        scratch_shapes=[pltpu.SemaphoreType.DMA((len(arrays),))],
        compiler_params=pltpu.CompilerParams(vmem_limit_bytes=1 << 20),
        name="resident",
    )(*kept_in(pltpu.HBM, *arrays))


def spread(source, start, target, at, sem):
    count, _, cut = target.shape
    size = source.shape[0]
    return [
        pltpu.make_async_copy(
            source.at[:, pl.ds(j * cut, cut)], target.at[j, pl.ds(at, size), :], sem
        )
        for j in range(count)
    ]


def pieces(chunk, rows, slot_rows):
    found = []
    row = chunk * rows
    while row < (chunk + 1) * rows:
        slot, offset = divmod(row, slot_rows)
        size = min(slot_rows - offset, (chunk + 1) * rows - row)
        found.append((slot, offset, row - chunk * rows, size))
        row += size
    return found


def fetch(fresh, fresh_here, arrived, target, sem):
    moved = pltpu.make_async_copy(arrived, target, sem)
    if fresh is None:
        moved.start()
        moved.wait()
        return

    @pl.when(fresh_here)
    def _():
        for source, at in fresh:
            for copy in spread(source, 0, target, at, sem):
                copy.start()
        moved.wait()

    @pl.when(jnp.logical_not(fresh_here))
    def _():
        moved.start()
        moved.wait()


def block(j, cut):
    return pl.ds(pl.multiple_of(j * cut, cut), cut)


def forward_kernel(
    tick, chunks, sections, place, plan, arrived, inputs, gain, w_in, w_out, *rest
):
    if tick > 0:
        rest = rest[5:]
    send, x_all, aux_all, hidden_all, w_in_t, w_out_t, *rest = rest
    x, aux, hidden, turned, sems = rest
    count, rows, cut = x.shape
    width = count * cut
    inner = w_in.shape[1]
    mine = tick - SKEW * place[0]
    active = jnp.logical_and(mine >= 0, mine < chunks)

    @pl.when(active)
    def _():
        fresh = None
        if tick < chunks:
            fresh = [
                (inputs.at[plan[slot], pl.ds(offset, size), :], at)
                for slot, offset, at, size in pieces(tick, rows, inputs.shape[1])
            ]
        fetch(fresh, place[0] == 0, arrived, x, sems.at[0])
        at = pl.ds(pl.multiple_of(mine * rows, rows), rows)
        store_x = pltpu.make_async_copy(x, x_all.at[:, at, :], sems.at[1])
        store_x.start()

        def project(j, carry):
            total, pre = carry
            value = x[j].astype(F32)
            piece = (value * gain[:, block(j, cut)]).astype(BF16)
            product = jnp.dot(piece, w_in[block(j, cut), :], preferred_element_type=F32)
            return total + value * value, pre + product

        start = jnp.zeros((rows, cut), F32), jnp.zeros((rows, inner), F32)
        total, pre = across(count, project, start)
        inverse = lax.rsqrt(jnp.sum(total, axis=1, keepdims=True) / width + EPSILON)
        pre = pre * inverse
        aux[:, :inner] = pre
        aux[:, inner:] = jnp.broadcast_to(inverse, (rows, AUX))
        store_aux = pltpu.make_async_copy(aux, aux_all.at[at, :], sems.at[2])
        store_aux.start()
        act = (pre / (1.0 + jnp.exp(-pre))).astype(BF16)
        hidden[...] = act
        store_hidden = pltpu.make_async_copy(hidden, hidden_all.at[at, :], sems.at[3])
        store_hidden.start()

        def expand(j, nothing):
            delta = jnp.dot(act, w_out[:, block(j, cut)], preferred_element_type=F32)
            send[j] = (x[j].astype(F32) + delta).astype(BF16)
            return nothing

        across(count, expand, 0)
        store_x.wait()
        store_aux.wait()
        store_hidden.wait()

    idle = SKEW * (sections - 1)

    def turn(j):
        turned[0] = w_in[block(j, cut), :].T
        first = pltpu.make_async_copy(turned.at[0], w_in_t.at[:, block(j, cut)], sems.at[4])
        first.start()
        turned[1] = w_out[:, block(j, cut)].T
        second = pltpu.make_async_copy(turned.at[1], w_out_t.at[block(j, cut), :], sems.at[5])
        second.start()
        first.wait()
        second.wait()

    spare = jnp.where(mine < 0, tick, tick - chunks)
    for again in range(-(-count // idle)):
        j = spare + again * idle

        @pl.when(jnp.logical_and(jnp.logical_not(active), j < count))
        def _():
            turn(j)


def forward_step(
    tick, chunks, rows, sections, count, place, plan, arrived, inputs, gain, w_in, w_out, kept
):
    width, inner = w_in.shape
    cut = width // count
    shapes = (
        jax.ShapeDtypeStruct((count, rows, cut), BF16),
        pltpu.HBM((count, chunks * rows, cut), BF16),
        pltpu.HBM((chunks * rows, inner + AUX), F32),
        pltpu.HBM((chunks * rows, inner), BF16),
        pltpu.HBM((inner, width), BF16),
        pltpu.HBM((width, inner), BF16),
    )
    specs = [smem(), smem(), hbm(), hbm(), vmem(), vmem(), vmem()] + [hbm()] * len(kept)
    return pl.pallas_call(
        functools.partial(forward_kernel, tick, chunks, sections),
        out_shape=shapes,
        in_specs=specs,
        out_specs=(vmem(),) + (hbm(),) * 5,
        scratch_shapes=[
            pltpu.VMEM((count, rows, cut), BF16),
            pltpu.VMEM((rows, inner + AUX), F32),
            pltpu.VMEM((rows, inner), BF16),
            pltpu.VMEM((2, inner, cut), BF16),
            pltpu.SemaphoreType.DMA((6,)),
        ],
        input_output_aliases={7 + k: 1 + k for k in range(len(kept))},
        compiler_params=pltpu.CompilerParams(vmem_limit_bytes=10 << 20),
        cost_estimate=pl.CostEstimate(
            flops=4 * rows * width * inner, bytes_accessed=10 << 20, transcendentals=0
        ),
        name="forward_step",
    )(
        place,
        plan,
        arrived,
        *kept_in(pltpu.HBM, inputs),
        gain,
        *kept_in(pltpu.VMEM, w_in, w_out),
        *kept_in(pltpu.HBM, *kept),
    )


def backward_kernel(
    tick, chunks, sections, held, parts, place, arrived, cotangent, x_all, aux_all, gain, w_in, w_out, *rest
):
    rest = rest[2 * held :]
    send, *rest = rest
    stores, rest = rest[: 2 * parts], rest[2 * parts :]
    up, x, aux, grad, sems = rest
    count, rows, cut = up.shape
    width = count * cut
    inner = w_in.shape[0]
    mine = tick - SKEW * (sections - 1 - place[0])
    active = jnp.logical_and(mine >= 0, mine < chunks)
    share = chunks // PARTS

    def put(value, which, sem):
        lead = PARTS - parts
        for part in range(parts):
            here = mine - (lead + part) * share

            def place_of():
                ref = stores[2 * part + which]
                at = pl.ds(pl.multiple_of(here * rows, rows), rows)
                return ref.at[:, at, :] if which == 0 else ref.at[at, :]

            @pl.when(jnp.logical_and(here >= 0, here < share))
            def _():
                pltpu.make_async_copy(value, place_of(), sem).start()

    @pl.when(active)
    def _():
        at = pl.ds(pl.multiple_of(mine * rows, rows), rows)
        load_x = pltpu.make_async_copy(x_all.at[:, at, :], x, sems.at[1])
        load_x.start()
        load_aux = pltpu.make_async_copy(aux_all.at[at, :], aux, sems.at[2])
        load_aux.start()
        fresh = None
        if tick < chunks:
            fresh = [
                (cotangent.at[slot, pl.ds(offset, size), :], at)
                for slot, offset, at, size in pieces(tick, rows, cotangent.shape[1])
            ]
        fetch(fresh, place[0] == sections - 1, arrived, up, sems.at[0])
        put(up, 0, sems.at[3])

        def project(j, total):
            return total + jnp.dot(up[j], w_out[block(j, cut), :], preferred_element_type=F32)

        grad_hidden = across(count, project, jnp.zeros((rows, inner), F32))
        load_aux.wait()
        pre = aux[:, :inner]
        inverse = aux[:, inner : inner + 1]
        gate = 1.0 / (1.0 + jnp.exp(-pre))
        exact = grad_hidden * gate * (1.0 + pre * (1.0 - gate))
        grad[...] = (exact * inverse).astype(BF16)
        put(grad, 1, sems.at[4])
        grad_pre = exact.astype(BF16)
        mean = jnp.sum(exact * pre, axis=1, keepdims=True) * (inverse / width)
        load_x.wait()

        def expand(j, nothing):
            cols = block(j, cut)
            back = jnp.dot(grad_pre, w_in[:, cols], preferred_element_type=F32)
            inside = back * gain[:, cols] - x[j].astype(F32) * mean
            send[j] = (up[j].astype(F32) + inverse * inside).astype(BF16)
            return nothing

        across(count, expand, 0)
        pltpu.make_async_copy(up, up, sems.at[3]).wait()
        pltpu.make_async_copy(grad, grad, sems.at[4]).wait()


def backward_step(
    tick, chunks, rows, sections, place, arrived, cotangent, x_all, aux_all, gain, w_in, w_out, kept, parts
):
    inner, width = w_in.shape
    count = x_all.shape[0]
    cut = width // count
    share = chunks // PARTS * rows
    shapes = [jax.ShapeDtypeStruct((count, rows, cut), BF16)]
    for _ in range(parts):
        shapes += [pltpu.HBM((count, share, cut), BF16), pltpu.HBM((share, inner), BF16)]
    specs = [smem()] + [hbm()] * 4 + [vmem()] * 3 + [hbm()] * len(kept)
    return pl.pallas_call(
        functools.partial(backward_kernel, tick, chunks, sections, len(kept) // 2, parts),
        out_shape=shapes,
        in_specs=specs,
        out_specs=[vmem()] + [hbm()] * (2 * parts),
        scratch_shapes=[
            pltpu.VMEM((count, rows, cut), BF16),
            pltpu.VMEM((count, rows, cut), BF16),
            pltpu.VMEM((rows, inner + AUX), F32),
            pltpu.VMEM((rows, inner), BF16),
            pltpu.SemaphoreType.DMA((5,)),
        ],
        input_output_aliases={8 + k: 1 + k for k in range(len(kept))},
        compiler_params=pltpu.CompilerParams(vmem_limit_bytes=10 << 20),
        cost_estimate=pl.CostEstimate(
            flops=4 * rows * width * inner, bytes_accessed=10 << 20, transcendentals=0
        ),
        name="backward_step",
    )(
        place,
        arrived,
        *kept_in(pltpu.HBM, cotangent, x_all, aux_all),
        gain,
        *kept_in(pltpu.VMEM, w_in, w_out),
        *kept_in(pltpu.HBM, *kept),
    )


def gathered(array, axis):
    return lax.all_gather(array, axis, axis=0, tiled=True)


def columns(array, axis):
    return lax.all_to_all(array, axis, split_axis=0, concat_axis=0, tiled=True)


def contracted(left, right):
    left = left.reshape(-1, left.shape[-1])
    right = right.reshape(-1, right.shape[-1])
    return lax.dot_general(left, right, (((0,), (0,)), ((), ())), preferred_element_type=F32)


def per_device(inputs, cotangent, plan_order, norm_gain, weight_in, weight_out):
    sections = lax.axis_size("pipe")
    count = lax.axis_size("dp")
    micro_count, row_count, width = inputs.shape
    chunks = CHUNKS
    rows = micro_count * row_count // chunks
    cut = width // count
    last = SKEW * (sections - 1)
    ticks = chunks + last
    onward = [(s, s + 1) for s in range(sections - 1)]
    back = [(s + 1, s) for s in range(sections - 1)]
    place = lax.axis_index("pipe").astype(jnp.int32).reshape(1)
    plan = plan_order.astype(jnp.int32)
    empty = jnp.zeros((count, rows, cut), BF16)

    w_in, w_out = resident(weight_in[0], weight_out[0])
    moving = {}
    kept = ()
    for tick in range(ticks):
        arrived = moving.pop(tick, empty)
        send, *kept = forward_step(
            tick,
            chunks,
            rows,
            sections,
            count,
            place,
            plan,
            arrived,
            inputs,
            norm_gain,
            w_in,
            w_out,
            kept,
        )
        if tick + SKEW < ticks:
            moving[tick + SKEW] = lax.ppermute(send, "pipe", onward)
    x_all, aux_all, hidden_all, w_in_t, w_out_t = kept
    x_cols = columns(x_all, "dp")
    hidden_rows = gathered(hidden_all, "dp")

    w_in, w_out = resident(w_in_t, w_out_t)
    share = chunks // PARTS
    moving = {}
    kept = []
    up_cols = []
    grad_rows = []
    for tick in range(ticks):
        arrived = moving.pop(tick, empty)
        if tick == TIED:
            arrived, x_cols = lax.optimization_barrier((arrived, x_cols))
        parts = PARTS - len(up_cols)
        send, *kept = backward_step(
            tick,
            chunks,
            rows,
            sections,
            place,
            arrived,
            cotangent,
            x_all,
            aux_all,
            norm_gain,
            w_in,
            w_out,
            kept,
            parts,
        )
        if tick + SKEW < ticks:
            moving[tick + SKEW] = lax.ppermute(send, "pipe", back)
        if tick - last + 1 == (len(up_cols) + 1) * share:
            up_cols.append(columns(kept[0], "dp"))
            grad_rows.append(gathered(kept[1], "dp"))
            kept = kept[2:]
    gain = lax.dynamic_slice(norm_gain[0], (lax.axis_index("dp") * cut,), (cut,))
    total_in = 0.0
    total_out = 0.0
    hidden_rows = hidden_rows.reshape(count, PARTS, share * rows, -1)
    x_cols = x_cols.reshape(count, PARTS, share * rows, -1)
    for part in range(PARTS):
        total_in = total_in + contracted(x_cols[:, part], grad_rows[part])
        total_out = total_out + contracted(hidden_rows[:, part], up_cols[part])
    total_in = (total_in * gain[:, None]).astype(BF16)
    return total_in[None], total_out.astype(BF16)[None]


def solution(mesh):
    in_specs = (
        P(None, "dp", None),
        P(None, "dp", None),
        P(),
        P("pipe", None),
        P("pipe", None, None),
        P("pipe", None, None),
    )
    out_specs = (P("pipe", "dp", None), P("pipe", None, "dp"))
    return jax.shard_map(
        per_device, mesh=mesh, in_specs=in_specs, out_specs=out_specs, check_vma=False
    )
```

time: 556 us -> 565 us (1.016)
  Pallas kernels: 262 us -> 120 us
  waiting for transfers between devices: 120 us -> 255 us
  starting transfers between devices: 119 us -> 138 us
  local copies, waits for them, and re-layouts: 24 us -> 13.5 us
    pallas_call x52 -> x44, Pallas kernels: 251 us -> 109 us  [the longest x22 72.8 us: forward_step(): pl.pallas_call(functools.partial(forward_kernel, tick, chunks, sections),...]
    ppermute x24 -> x20, waiting for transfers between devices: 33 us -> 149 us  [per_device(): moving[tick + SKEW] = lax.ppermute(send, 'pipe', back)]
    all_to_all x2 -> x3, waiting for transfers between devices: 85.8 us -> 40.6 us  [columns(): return lax.all_to_all(array, axis, split_axis=0, concat_axis=0, tiled=True)]
    all_gather x2 -> x3, waiting for transfers between devices: 0.01 us -> 38.3 us  [gathered(): return lax.all_gather(array, axis, axis=0, tiled=True)]
    ppermute x24 -> x20, waiting for transfers between devices: 0.06 us -> 26.4 us  [per_device(): moving[tick + SKEW] = lax.ppermute(send, 'pipe', onward)]
    ppermute x24 -> x20, starting transfers between devices: 50.8 us -> 75.9 us  [per_device(): moving[tick + SKEW] = lax.ppermute(send, 'pipe', onward)]
    unnamed x10 -> x18, local copies, waits for them, and re-layouts: 24 us -> 6.79 us
    slice x0 -> x2, local copies, waits for them, and re-layouts: none -> 6.71 us  [the longest x1 3.37 us: per_device(): total_in = total_in + contracted(x_cols[:, part], grad_rows[part])]
  transfers between devices with their start and end apart: 52 -> 46, of which waited for: 25 -> 37; matrix products, arithmetic and copies ran while one was open for 5% -> 3% of each run, Pallas kernels for 45% -> 19%
where the time goes in v3:
time: 565 us; the launch traced here: 555 us
  waiting for transfers between devices  255 us (45%)
  starting transfers between devices  138 us (24%)
  Pallas kernels  120 us (21%)
  between operations  14.8 us (3%)
  local copies, waits for them, and re-layouts  13.5 us (2%)
  matrix products  13 us (2%)
    ppermute x20, waiting for transfers between devices, per_device(): moving[tick + SKEW] = lax.ppermute(send, 'pipe', back)  149 us
    ppermute x20, starting transfers between devices, per_device(): moving[tick + SKEW] = lax.ppermute(send, 'pipe', onward)  75.9 us
    pallas_call x22, Pallas kernels, forward_step(): pl.pallas_call(functools.partial(forward_kernel, tick, chunks, sections),...  72.8 us
    all_to_all x3, waiting for transfers between devices, columns(): return lax.all_to_all(array, axis, split_axis=0, concat_axis=0, tiled=True)  40.6 us
    all_gather x3, waiting for transfers between devices, gathered(): return lax.all_gather(array, axis, axis=0, tiled=True)  38.3 us
    all_to_all x3, starting transfers between devices, columns(): return lax.all_to_all(array, axis, split_axis=0, concat_axis=0, tiled=True)  36.3 us
    pallas_call x22, Pallas kernels, backward_step(): pl.pallas_call(functools.partial(backward_kernel, tick, chunks, sections,...  35.9 us
    ppermute x20, waiting for transfers between devices, per_device(): moving[tick + SKEW] = lax.ppermute(send, 'pipe', onward)  26.4 us
  transfers between devices with their start and end apart: 46, of which 37 were waited for; matrix products, arithmetic and copies ran while one was open for 3% of the time, Pallas kernels for 19%

profile of v3, /device:TPU:1, one launch (start us, length us, event | category | flops | bytes accessed | tf_op | source)
XLA Modules:
  0.0 554.5 jit_solution(5986287042891841269)
XLA Ops:
  7.2 5.8 %resident.2 = (bf16[8192,512]{1,0:T(8,128)(2,1)S(1)}, bf16[512,8192]{1,0:T(8,128)(2,1)S(1)}) custom-call(bf16[8192,512]{1,0:T(8,128)(2,1)} %bitcast.24, bf16[512,8192]{1,0:T(8,128)(2,1)} %bitcast.25), custom_call_target="tpu_custom_call" | custom-call | tf_op jit(solution)/shard_map/resident/pallas_call | solution.py:61
  13.1 5.4 forward_step.22
  20.2 5.5 forward_step.23
  27.7 5.4 forward_step.24
  36.5 5.4 forward_step.25
  44.9 5.4 forward_step.26
  52.1 5.5 forward_step.27
  61.6 5.4 forward_step.28
  70.2 5.4 forward_step.29
  80.1 6.3 %collective-permute-start.9 = (bf16[16,24,512]{2,1,0:T(8,128)(2,1)S(1)}, bf16[16,24,512]{2,1,0:T(8,128)(2,1)S(1)}, u32[]{:S(2)}, u32[]{:S(2)}) collective-permute-start(bf16[16,24,512]{2,1,0:T(8,128)(2,1)S(1)} %get-tuple-element.294), channel_id=1, source_target_pairs={{0,16},{16,32},{32,48},{48,64},{64,80},{80,96},{96,112},{1,17},{17... | collective-permute-start | bytes 1179656 | tf_op jit(solution)/shard_map/ppermute | solution.py:398
  89.5 5.6 %collective-permute-start.8 = (bf16[16,24,512]{2,1,0:T(8,128)(2,1)S(1)}, bf16[16,24,512]{2,1,0:T(8,128)(2,1)S(1)}, u32[]{:S(2)}, u32[]{:S(2)}) collective-permute-start(bf16[16,24,512]{2,1,0:T(8,128)(2,1)S(1)} %get-tuple-element.293), channel_id=1, source_target_pairs={{0,16},{16,32},{32,48},{48,64},{64,80},{80,96},{96,112},{1,17},{17... | collective-permute-start | bytes 1179656 | tf_op jit(solution)/shard_map/ppermute | solution.py:398
  103.6 5.1 collective-permute-start.10
  180.2 5.9 %collective-permute-done.18.arrived = bf16[16,24,512]{2,1,0:T(8,128)(2,1)S(1)} collective-permute-done((bf16[16,24,512]{2,1,0:T(8,128)(2,1)S(1)}, bf16[16,24,512]{2,1,0:T(8,128)(2,1)S(1)}, u32[]{:S(2)}, u32[]{:S(2)}) %collective-permute-start.18) | collective-permute-done | bytes 393248 | tf_op jit(solution)/shard_map/ppermute | solution.py:398
  188.6 12.0 %all-to-all-start = ((bf16[16,192,512]{2,1,0:T(8,128)(2,1)}), bf16[16,192,512]{2,1,0:T(8,128)(2,1)}, u32[]{:S(2)}, u32[]{:S(2)}) async-start(bf16[16,192,512]{2,1,0:T(8,128)(2,1)} %get-tuple-element.365.x_all), calls=%async_computation | async-start | bytes 6291456 | tf_op jit(solution)/shard_map/all_to_all | solution.py:353
  200.7 5.8 %resident.3 = (bf16[512,8192]{1,0:T(8,128)(2,1)S(1)}, bf16[8192,512]{1,0:T(8,128)(2,1)S(1)}) custom-call(bf16[512,8192]{1,0:T(8,128)(2,1)} %get-tuple-element.367.refs_0_, bf16[8192,512]{1,0:T(8,128)(2,1)} %get-tuple-element.368.refs_1_), custom_call_target="tpu_custom_call" | custom-call | tf_op jit(solution)/shard_map/resident/pallas_call | solution.py:61
  209.5 40.1 %collective-permute-done.20.arrived = bf16[16,24,512]{2,1,0:T(8,128)(2,1)S(1)} collective-permute-done((bf16[16,24,512]{2,1,0:T(8,128)(2,1)S(1)}, bf16[16,24,512]{2,1,0:T(8,128)(2,1)S(1)}, u32[]{:S(2)}, u32[]{:S(2)}) %collective-permute-start.20) | collective-permute-done | bytes 393248 | tf_op jit(solution)/shard_map/ppermute | solution.py:431
  250.9 9.1 %collective-permute-done.22.arrived = bf16[16,24,512]{2,1,0:T(8,128)(2,1)S(1)} collective-permute-done((bf16[16,24,512]{2,1,0:T(8,128)(2,1)S(1)}, bf16[16,24,512]{2,1,0:T(8,128)(2,1)S(1)}, u32[]{:S(2)}, u32[]{:S(2)}) %collective-permute-start.22) | collective-permute-done | bytes 393248 | tf_op jit(solution)/shard_map/ppermute | solution.py:431
  261.3 13.6 %collective-permute-done.21.arrived = bf16[16,24,512]{2,1,0:T(8,128)(2,1)S(1)} collective-permute-done((bf16[16,24,512]{2,1,0:T(8,128)(2,1)S(1)}, bf16[16,24,512]{2,1,0:T(8,128)(2,1)S(1)}, u32[]{:S(2)}, u32[]{:S(2)}) %collective-permute-start.21) | collective-permute-done | bytes 393248 | tf_op jit(solution)/shard_map/ppermute | solution.py:431
  276.3 7.1 %collective-permute-done.24.arrived = bf16[16,24,512]{2,1,0:T(8,128)(2,1)S(1)} collective-permute-done((bf16[16,24,512]{2,1,0:T(8,128)(2,1)S(1)}, bf16[16,24,512]{2,1,0:T(8,128)(2,1)S(1)}, u32[]{:S(2)}, u32[]{:S(2)}) %collective-permute-start.24) | collective-permute-done | bytes 393248 | tf_op jit(solution)/shard_map/ppermute | solution.py:431
  284.7 7.1 %collective-permute-done.23.arrived = bf16[16,24,512]{2,1,0:T(8,128)(2,1)S(1)} collective-permute-done((bf16[16,24,512]{2,1,0:T(8,128)(2,1)S(1)}, bf16[16,24,512]{2,1,0:T(8,128)(2,1)S(1)}, u32[]{:S(2)}, u32[]{:S(2)}) %collective-permute-start.23) | collective-permute-done | bytes 393248 | tf_op jit(solution)/shard_map/ppermute | solution.py:431
  293.2 7.0 %collective-permute-done.26.arrived = bf16[16,24,512]{2,1,0:T(8,128)(2,1)S(1)} collective-permute-done((bf16[16,24,512]{2,1,0:T(8,128)(2,1)S(1)}, bf16[16,24,512]{2,1,0:T(8,128)(2,1)S(1)}, u32[]{:S(2)}, u32[]{:S(2)}) %collective-permute-start.26) | collective-permute-done | bytes 393248 | tf_op jit(solution)/shard_map/ppermute | solution.py:431
  301.5 7.1 %collective-permute-done.25.arrived = bf16[16,24,512]{2,1,0:T(8,128)(2,1)S(1)} collective-permute-done((bf16[16,24,512]{2,1,0:T(8,128)(2,1)S(1)}, bf16[16,24,512]{2,1,0:T(8,128)(2,1)S(1)}, u32[]{:S(2)}, u32[]{:S(2)}) %collective-permute-start.25) | collective-permute-done | bytes 393248 | tf_op jit(solution)/shard_map/ppermute | solution.py:431
  309.9 7.1 %collective-permute-done.28.arrived = bf16[16,24,512]{2,1,0:T(8,128)(2,1)S(1)} collective-permute-done((bf16[16,24,512]{2,1,0:T(8,128)(2,1)S(1)}, bf16[16,24,512]{2,1,0:T(8,128)(2,1)S(1)}, u32[]{:S(2)}, u32[]{:S(2)}) %collective-permute-start.28) | collective-permute-done | bytes 393248 | tf_op jit(solution)/shard_map/ppermute | solution.py:431
  318.3 7.1 %collective-permute-done.27.arrived = bf16[16,24,512]{2,1,0:T(8,128)(2,1)S(1)} collective-permute-done((bf16[16,24,512]{2,1,0:T(8,128)(2,1)S(1)}, bf16[16,24,512]{2,1,0:T(8,128)(2,1)S(1)}, u32[]{:S(2)}, u32[]{:S(2)}) %collective-permute-start.27) | collective-permute-done | bytes 393248 | tf_op jit(solution)/shard_map/ppermute | solution.py:431
  326.8 7.1 %collective-permute-done.30.arrived = bf16[16,24,512]{2,1,0:T(8,128)(2,1)S(1)} collective-permute-done((bf16[16,24,512]{2,1,0:T(8,128)(2,1)S(1)}, bf16[16,24,512]{2,1,0:T(8,128)(2,1)S(1)}, u32[]{:S(2)}, u32[]{:S(2)}) %collective-permute-start.30) | collective-permute-done | bytes 393248 | tf_op jit(solution)/shard_map/ppermute | solution.py:431
  335.2 7.1 %collective-permute-done.29.arrived = bf16[16,24,512]{2,1,0:T(8,128)(2,1)S(1)} collective-permute-done((bf16[16,24,512]{2,1,0:T(8,128)(2,1)S(1)}, bf16[16,24,512]{2,1,0:T(8,128)(2,1)S(1)}, u32[]{:S(2)}, u32[]{:S(2)}) %collective-permute-start.29) | collective-permute-done | bytes 393248 | tf_op jit(solution)/shard_map/ppermute | solution.py:431
  352.0 10.1 %collective-permute-done.33.arrived = bf16[16,24,512]{2,1,0:T(8,128)(2,1)S(1)} collective-permute-done((bf16[16,24,512]{2,1,0:T(8,128)(2,1)S(1)}, bf16[16,24,512]{2,1,0:T(8,128)(2,1)S(1)}, u32[]{:S(2)}, u32[]{:S(2)}) %collective-permute-start.33) | collective-permute-done | bytes 393248 | tf_op jit(solution)/shard_map/ppermute | solution.py:431
  424.2 18.7 %all-to-all-start.2 = ((bf16[16,96,512]{2,1,0:T(8,128)(2,1)}), bf16[16,96,512]{2,1,0:T(8,128)(2,1)S(1)}, u32[]{:S(2)}, u32[]{:S(2)}) async-start(bf16[16,96,512]{2,1,0:T(8,128)(2,1)} %get-tuple-element.473), calls=%async_computation.2 | async-start | bytes 3145728 | tf_op jit(solution)/shard_map/all_to_all | solution.py:353
  443.6 23.1 %all-to-all-done.2 = bf16[16,96,512]{2,1,0:T(8,128)(2,1)S(1)} async-done(((bf16[16,96,512]{2,1,0:T(8,128)(2,1)}), bf16[16,96,512]{2,1,0:T(8,128)(2,1)S(1)}, u32[]{:S(2)}, u32[]{:S(2)}) %all-to-all-start.2) | async-done | bytes 1572896 | tf_op jit(solution)/shard_map/all_to_all | solution.py:353
  466.7 5.6 %all-to-all-start.1 = ((bf16[16,96,512]{2,1,0:T(8,128)(2,1)}), bf16[16,96,512]{2,1,0:T(8,128)(2,1)}, u32[]{:S(2)}, u32[]{:S(2)}) async-start(bf16[16,96,512]{2,1,0:T(8,128)(2,1)} %get-tuple-element.472), calls=%async_computation.1 | async-start | bytes 3145728 | tf_op jit(solution)/shard_map/all_to_all | solution.py:353
  481.0 17.4 %all-to-all-done.1 = bf16[16,96,512]{2,1,0:T(8,128)(2,1)} async-done(((bf16[16,96,512]{2,1,0:T(8,128)(2,1)}), bf16[16,96,512]{2,1,0:T(8,128)(2,1)}, u32[]{:S(2)}, u32[]{:S(2)}) %all-to-all-start.1) | async-done | bytes 1572896 | tf_op jit(solution)/shard_map/all_to_all | solution.py:353
  506.0 38.3 %all-gather.4.cloned.1.call-done = bf16[1536,512]{1,0:T(8,128)(2,1)} async-done(((bf16[96,512]{1,0:T(8,128)(2,1)}), bf16[1536,512]{1,0:T(8,128)(2,1)}) %all-gather.4.cloned.1.call-update) | async-done | bytes 1572880 | tf_op jit(solution)/shard_map/all_gather | solution.py:349
  (135 shorter events, 217.3 us)
Async XLA Ops:
  7.2 468.5 %all-gather.8.cloned.1.call-start = ((), (), s32[]{:S(2)}) async-start(), calls=%async_computation.5 | async-start | bytes 3342336 | tf_op jit(solution)/shard_map/all_gather | solution.py:349
  80.1 15.0 %collective-permute-start.9 = (bf16[16,24,512]{2,1,0:T(8,128)(2,1)S(1)}, bf16[16,24,512]{2,1,0:T(8,128)(2,1)S(1)}, u32[]{:S(2)}, u32[]{:S(2)}) collective-permute-start(bf16[16,24,512]{2,1,0:T(8,128)(2,1)S(1)} %get-tuple-element.294), channel_id=1, source_target_pairs={{0,16},{16,32},{32,48},{48,64},{64,80},{80,96},{96,112},{1,17},{17... | collective-permute-start | bytes 1179656 | tf_op jit(solution)/shard_map/ppermute | solution.py:398
  97.0 13.2 %collective-permute-start.11 = (bf16[16,24,512]{2,1,0:T(8,128)(2,1)S(1)}, bf16[16,24,512]{2,1,0:T(8,128)(2,1)S(1)}, u32[]{:S(2)}, u32[]{:S(2)}) collective-permute-start(bf16[16,24,512]{2,1,0:T(8,128)(2,1)S(1)} %get-tuple-element.306), channel_id=1, source_target_pairs={{0,16},{16,32},{32,48},{48,64},{64,80},{80,96},{96,112},{1,17},{17... | collective-permute-start | bytes 1179656 | tf_op jit(solution)/shard_map/ppermute | solution.py:398
  103.6 15.0 %collective-permute-start.10 = (bf16[16,24,512]{2,1,0:T(8,128)(2,1)S(1)}, bf16[16,24,512]{2,1,0:T(8,128)(2,1)S(1)}, u32[]{:S(2)}, u32[]{:S(2)}) collective-permute-start(bf16[16,24,512]{2,1,0:T(8,128)(2,1)S(1)} %get-tuple-element.305), channel_id=1, source_target_pairs={{0,16},{16,32},{32,48},{48,64},{64,80},{80,96},{96,112},{1,17},{17... | collective-permute-start | bytes 1179656 | tf_op jit(solution)/shard_map/ppermute | solution.py:398
  112.0 15.0 %collective-permute-start.13 = (bf16[16,24,512]{2,1,0:T(8,128)(2,1)S(1)}, bf16[16,24,512]{2,1,0:T(8,128)(2,1)S(1)}, u32[]{:S(2)}, u32[]{:S(2)}) collective-permute-start(bf16[16,24,512]{2,1,0:T(8,128)(2,1)S(1)} %get-tuple-element.318), channel_id=1, source_target_pairs={{0,16},{16,32},{32,48},{48,64},{64,80},{80,96},{96,112},{1,17},{17... | collective-permute-start | bytes 1179656 | tf_op jit(solution)/shard_map/ppermute | solution.py:398
  120.5 15.0 %collective-permute-start.12 = (bf16[16,24,512]{2,1,0:T(8,128)(2,1)S(1)}, bf16[16,24,512]{2,1,0:T(8,128)(2,1)S(1)}, u32[]{:S(2)}, u32[]{:S(2)}) collective-permute-start(bf16[16,24,512]{2,1,0:T(8,128)(2,1)S(1)} %get-tuple-element.317), channel_id=1, source_target_pairs={{0,16},{16,32},{32,48},{48,64},{64,80},{80,96},{96,112},{1,17},{17... | collective-permute-start | bytes 1179656 | tf_op jit(solution)/shard_map/ppermute | solution.py:398
  128.9 15.1 %collective-permute-start.15 = (bf16[16,24,512]{2,1,0:T(8,128)(2,1)S(1)}, bf16[16,24,512]{2,1,0:T(8,128)(2,1)S(1)}, u32[]{:S(2)}, u32[]{:S(2)}) collective-permute-start(bf16[16,24,512]{2,1,0:T(8,128)(2,1)S(1)} %get-tuple-element.330), channel_id=1, source_target_pairs={{0,16},{16,32},{32,48},{48,64},{64,80},{80,96},{96,112},{1,17},{17... | collective-permute-start | bytes 1179656 | tf_op jit(solution)/shard_map/ppermute | solution.py:398
  137.3 15.0 %collective-permute-start.14 = (bf16[16,24,512]{2,1,0:T(8,128)(2,1)S(1)}, bf16[16,24,512]{2,1,0:T(8,128)(2,1)S(1)}, u32[]{:S(2)}, u32[]{:S(2)}) collective-permute-start(bf16[16,24,512]{2,1,0:T(8,128)(2,1)S(1)} %get-tuple-element.329), channel_id=1, source_target_pairs={{0,16},{16,32},{32,48},{48,64},{64,80},{80,96},{96,112},{1,17},{17... | collective-permute-start | bytes 1179656 | tf_op jit(solution)/shard_map/ppermute | solution.py:398
  145.7 15.1 %collective-permute-start.17 = (bf16[16,24,512]{2,1,0:T(8,128)(2,1)S(1)}, bf16[16,24,512]{2,1,0:T(8,128)(2,1)S(1)}, u32[]{:S(2)}, u32[]{:S(2)}) collective-permute-start(bf16[16,24,512]{2,1,0:T(8,128)(2,1)S(1)} %get-tuple-element.342), channel_id=1, source_target_pairs={{0,16},{16,32},{32,48},{48,64},{64,80},{80,96},{96,112},{1,17},{17... | collective-permute-start | bytes 1179656 | tf_op jit(solution)/shard_map/ppermute | solution.py:398
  154.2 15.0 %collective-permute-start.16 = (bf16[16,24,512]{2,1,0:T(8,128)(2,1)S(1)}, bf16[16,24,512]{2,1,0:T(8,128)(2,1)S(1)}, u32[]{:S(2)}, u32[]{:S(2)}) collective-permute-start(bf16[16,24,512]{2,1,0:T(8,128)(2,1)S(1)} %get-tuple-element.341), channel_id=1, source_target_pairs={{0,16},{16,32},{32,48},{48,64},{64,80},{80,96},{96,112},{1,17},{17... | collective-permute-start | bytes 1179656 | tf_op jit(solution)/shard_map/ppermute | solution.py:398
  162.6 15.0 %collective-permute-start.19 = (bf16[16,24,512]{2,1,0:T(8,128)(2,1)S(1)}, bf16[16,24,512]{2,1,0:T(8,128)(2,1)S(1)}, u32[]{:S(2)}, u32[]{:S(2)}) collective-permute-start(bf16[16,24,512]{2,1,0:T(8,128)(2,1)S(1)} %get-tuple-element.354), channel_id=1, source_target_pairs={{0,16},{16,32},{32,48},{48,64},{64,80},{80,96},{96,112},{1,17},{17... | collective-permute-start | bytes 1179656 | tf_op jit(solution)/shard_map/ppermute | solution.py:398
  171.0 15.0 %collective-permute-start.18 = (bf16[16,24,512]{2,1,0:T(8,128)(2,1)S(1)}, bf16[16,24,512]{2,1,0:T(8,128)(2,1)S(1)}, u32[]{:S(2)}, u32[]{:S(2)}) collective-permute-start(bf16[16,24,512]{2,1,0:T(8,128)(2,1)S(1)} %get-tuple-element.353), channel_id=1, source_target_pairs={{0,16},{16,32},{32,48},{48,64},{64,80},{80,96},{96,112},{1,17},{17... | collective-permute-start | bytes 1179656 | tf_op jit(solution)/shard_map/ppermute | solution.py:398
  188.6 153.6 %all-to-all-start = ((bf16[16,192,512]{2,1,0:T(8,128)(2,1)}), bf16[16,192,512]{2,1,0:T(8,128)(2,1)}, u32[]{:S(2)}, u32[]{:S(2)}) async-start(bf16[16,192,512]{2,1,0:T(8,128)(2,1)} %get-tuple-element.365.x_all), calls=%async_computation | async-start | bytes 6291456 | tf_op jit(solution)/shard_map/all_to_all | solution.py:353
  200.7 301.8 %all-gather.6.cloned.1.call-start = ((), (), s32[]{:S(2)}) async-start(), calls=%async_computation.4 | async-start | bytes 1671168 | tf_op jit(solution)/shard_map/all_gather | solution.py:349
  206.7 42.9 %collective-permute-start.20 = (bf16[16,24,512]{2,1,0:T(8,128)(2,1)S(1)}, bf16[16,24,512]{2,1,0:T(8,128)(2,1)S(1)}, u32[]{:S(2)}, u32[]{:S(2)}) collective-permute-start(bf16[16,24,512]{2,1,0:T(8,128)(2,1)S(1)} %get-tuple-element.371), channel_id=1, source_target_pairs={{16,0},{32,16},{48,32},{64,48},{80,64},{96,80},{112,96},{17,1},{33... | collective-permute-start | bytes 1179656 | tf_op jit(solution)/shard_map/ppermute | solution.py:431
  208.2 51.8 %collective-permute-start.22 = (bf16[16,24,512]{2,1,0:T(8,128)(2,1)S(1)}, bf16[16,24,512]{2,1,0:T(8,128)(2,1)S(1)}, u32[]{:S(2)}, u32[]{:S(2)}) collective-permute-start(bf16[16,24,512]{2,1,0:T(8,128)(2,1)S(1)} %get-tuple-element.381), channel_id=1, source_target_pairs={{16,0},{32,16},{48,32},{64,48},{80,64},{96,80},{112,96},{17,1},{33... | collective-permute-start | bytes 1179656 | tf_op jit(solution)/shard_map/ppermute | solution.py:431
  249.6 25.3 %collective-permute-start.21 = (bf16[16,24,512]{2,1,0:T(8,128)(2,1)S(1)}, bf16[16,24,512]{2,1,0:T(8,128)(2,1)S(1)}, u32[]{:S(2)}, u32[]{:S(2)}) collective-permute-start(bf16[16,24,512]{2,1,0:T(8,128)(2,1)S(1)} %get-tuple-element.380), channel_id=1, source_target_pairs={{16,0},{32,16},{48,32},{64,48},{80,64},{96,80},{112,96},{17,1},{33... | collective-permute-start | bytes 1179656 | tf_op jit(solution)/shard_map/ppermute | solution.py:431
  260.0 23.3 %collective-permute-start.24 = (bf16[16,24,512]{2,1,0:T(8,128)(2,1)S(1)}, bf16[16,24,512]{2,1,0:T(8,128)(2,1)S(1)}, u32[]{:S(2)}, u32[]{:S(2)}) collective-permute-start(bf16[16,24,512]{2,1,0:T(8,128)(2,1)S(1)} %get-tuple-element.391), channel_id=1, source_target_pairs={{16,0},{32,16},{48,32},{64,48},{80,64},{96,80},{112,96},{17,1},{33... | collective-permute-start | bytes 1179656 | tf_op jit(solution)/shard_map/ppermute | solution.py:431
  275.0 16.8 %collective-permute-start.23 = (bf16[16,24,512]{2,1,0:T(8,128)(2,1)S(1)}, bf16[16,24,512]{2,1,0:T(8,128)(2,1)S(1)}, u32[]{:S(2)}, u32[]{:S(2)}) collective-permute-start(bf16[16,24,512]{2,1,0:T(8,128)(2,1)S(1)} %get-tuple-element.390), channel_id=1, source_target_pairs={{16,0},{32,16},{48,32},{64,48},{80,64},{96,80},{112,96},{17,1},{33... | collective-permute-start | bytes 1179656 | tf_op jit(solution)/shard_map/ppermute | solution.py:431
  283.4 16.7 %collective-permute-start.26 = (bf16[16,24,512]{2,1,0:T(8,128)(2,1)S(1)}, bf16[16,24,512]{2,1,0:T(8,128)(2,1)S(1)}, u32[]{:S(2)}, u32[]{:S(2)}) collective-permute-start(bf16[16,24,512]{2,1,0:T(8,128)(2,1)S(1)} %get-tuple-element.401), channel_id=1, source_target_pairs={{16,0},{32,16},{48,32},{64,48},{80,64},{96,80},{112,96},{17,1},{33... | collective-permute-start | bytes 1179656 | tf_op jit(solution)/shard_map/ppermute | solution.py:431
  291.9 16.7 %collective-permute-start.25 = (bf16[16,24,512]{2,1,0:T(8,128)(2,1)S(1)}, bf16[16,24,512]{2,1,0:T(8,128)(2,1)S(1)}, u32[]{:S(2)}, u32[]{:S(2)}) collective-permute-start(bf16[16,24,512]{2,1,0:T(8,128)(2,1)S(1)} %get-tuple-element.400), channel_id=1, source_target_pairs={{16,0},{32,16},{48,32},{64,48},{80,64},{96,80},{112,96},{17,1},{33... | collective-permute-start | bytes 1179656 | tf_op jit(solution)/shard_map/ppermute | solution.py:431
  300.2 16.8 %collective-permute-start.28 = (bf16[16,24,512]{2,1,0:T(8,128)(2,1)S(1)}, bf16[16,24,512]{2,1,0:T(8,128)(2,1)S(1)}, u32[]{:S(2)}, u32[]{:S(2)}) collective-permute-start(bf16[16,24,512]{2,1,0:T(8,128)(2,1)S(1)} %get-tuple-element.411), channel_id=1, source_target_pairs={{16,0},{32,16},{48,32},{64,48},{80,64},{96,80},{112,96},{17,1},{33... | collective-permute-start | bytes 1179656 | tf_op jit(solution)/shard_map/ppermute | solution.py:431
  308.6 16.8 %collective-permute-start.27 = (bf16[16,24,512]{2,1,0:T(8,128)(2,1)S(1)}, bf16[16,24,512]{2,1,0:T(8,128)(2,1)S(1)}, u32[]{:S(2)}, u32[]{:S(2)}) collective-permute-start(bf16[16,24,512]{2,1,0:T(8,128)(2,1)S(1)} %get-tuple-element.410), channel_id=1, source_target_pairs={{16,0},{32,16},{48,32},{64,48},{80,64},{96,80},{112,96},{17,1},{33... | collective-permute-start | bytes 1179656 | tf_op jit(solution)/shard_map/ppermute | solution.py:431
  317.0 16.8 %collective-permute-start.30 = (bf16[16,24,512]{2,1,0:T(8,128)(2,1)S(1)}, bf16[16,24,512]{2,1,0:T(8,128)(2,1)S(1)}, u32[]{:S(2)}, u32[]{:S(2)}) collective-permute-start(bf16[16,24,512]{2,1,0:T(8,128)(2,1)S(1)} %get-tuple-element.422), channel_id=1, source_target_pairs={{16,0},{32,16},{48,32},{64,48},{80,64},{96,80},{112,96},{17,1},{33... | collective-permute-start | bytes 1179656 | tf_op jit(solution)/shard_map/ppermute | solution.py:431
  325.5 16.8 %collective-permute-start.29 = (bf16[16,24,512]{2,1,0:T(8,128)(2,1)S(1)}, bf16[16,24,512]{2,1,0:T(8,128)(2,1)S(1)}, u32[]{:S(2)}, u32[]{:S(2)}) collective-permute-start(bf16[16,24,512]{2,1,0:T(8,128)(2,1)S(1)} %get-tuple-element.420), channel_id=1, source_target_pairs={{16,0},{32,16},{48,32},{64,48},{80,64},{96,80},{112,96},{17,1},{33... | collective-permute-start | bytes 1179656 | tf_op jit(solution)/shard_map/ppermute | solution.py:431
  333.9 16.8 %collective-permute-start.31 = (bf16[16,24,512]{2,1,0:T(8,128)(2,1)S(1)}, bf16[16,24,512]{2,1,0:T(8,128)(2,1)S(1)}, u32[]{:S(2)}, u32[]{:S(2)}) collective-permute-start(bf16[16,24,512]{2,1,0:T(8,128)(2,1)S(1)} %get-tuple-element.427), channel_id=1, source_target_pairs={{16,0},{32,16},{48,32},{64,48},{80,64},{96,80},{112,96},{17,1},{33... | collective-permute-start | bytes 1179656 | tf_op jit(solution)/shard_map/ppermute | solution.py:431
  350.7 19.8 %collective-permute-start.32 = (bf16[16,24,512]{2,1,0:T(8,128)(2,1)S(1)}, bf16[16,24,512]{2,1,0:T(8,128)(2,1)S(1)}, u32[]{:S(2)}, u32[]{:S(2)}) collective-permute-start(bf16[16,24,512]{2,1,0:T(8,128)(2,1)S(1)} %get-tuple-element.437), channel_id=1, source_target_pairs={{16,0},{32,16},{48,32},{64,48},{80,64},{96,80},{112,96},{17,1},{33... | collective-permute-start | bytes 1179656 | tf_op jit(solution)/shard_map/ppermute | solution.py:431
  381.0 13.7 %collective-permute-start.37 = (bf16[16,24,512]{2,1,0:T(8,128)(2,1)S(1)}, bf16[16,24,512]{2,1,0:T(8,128)(2,1)S(1)}, u32[]{:S(2)}, u32[]{:S(2)}) collective-permute-start(bf16[16,24,512]{2,1,0:T(8,128)(2,1)S(1)} %get-tuple-element.459), channel_id=1, source_target_pairs={{16,0},{32,16},{48,32},{64,48},{80,64},{96,80},{112,96},{17,1},{33... | collective-permute-start | bytes 1179656 | tf_op jit(solution)/shard_map/ppermute | solution.py:431
  405.9 13.4 %collective-permute-start.38 = (bf16[16,24,512]{2,1,0:T(8,128)(2,1)S(1)}, bf16[16,24,512]{2,1,0:T(8,128)(2,1)S(1)}, u32[]{:S(2)}, u32[]{:S(2)}) collective-permute-start(bf16[16,24,512]{2,1,0:T(8,128)(2,1)S(1)} %get-tuple-element.464), channel_id=1, source_target_pairs={{16,0},{32,16},{48,32},{64,48},{80,64},{96,80},{112,96},{17,1},{33... | collective-permute-start | bytes 1179656 | tf_op jit(solution)/shard_map/ppermute | solution.py:431
  424.2 42.5 %all-to-all-start.2 = ((bf16[16,96,512]{2,1,0:T(8,128)(2,1)}), bf16[16,96,512]{2,1,0:T(8,128)(2,1)S(1)}, u32[]{:S(2)}, u32[]{:S(2)}) async-start(bf16[16,96,512]{2,1,0:T(8,128)(2,1)} %get-tuple-element.473), calls=%async_computation.2 | async-start | bytes 3145728 | tf_op jit(solution)/shard_map/all_to_all | solution.py:353
  442.8 101.4 %all-gather.4.cloned.1.call-start = ((), (), s32[]{:S(2)}) async-start(), calls=%async_computation.3 | async-start | bytes 1671168 | tf_op jit(solution)/shard_map/all_gather | solution.py:349
  466.7 31.8 %all-to-all-start.1 = ((bf16[16,96,512]{2,1,0:T(8,128)(2,1)}), bf16[16,96,512]{2,1,0:T(8,128)(2,1)}, u32[]{:S(2)}, u32[]{:S(2)}) async-start(bf16[16,96,512]{2,1,0:T(8,128)(2,1)} %get-tuple-element.472), calls=%async_computation.1 | async-start | bytes 3145728 | tf_op jit(solution)/shard_map/all_to_all | solution.py:353
  (23 other events, 486.1 us)
Sparse Core Ops, SparseCore 0:
  188.8 152.7 all-gather.7
  424.3 70.5 all-gather.5
  497.4 46.8 all-gather.3
